TPU v7x, 32 devices: a whole 2x2x4 slice. The times are simulated.
32 devices in a mesh: comp: 4 (over y, x), cell: 8 (over z, core).
Axes of the slice: x: 2, y: 2, z: 4, core: 2. Of those that a mesh axis runs over, the one named last changes fastest.
Arguments:
- biomass: float32 [48, 64, 4096], P(None, None, ('comp', 'cell')), may hold values from 0.1 to 2
- patch_area: float32 [48, 4096], P(None, ('comp', 'cell')), may hold values from 0.005 to 0.04
- cohort_traits: float32 [4, 64], replicated, may hold values from 0.1 to 1
- cell_forcing: float32 [5, 4096], P(None, ('comp', 'cell')), may hold values from 0.1 to 1
- disturb_weight: float32 [4, 4096], P(None, ('comp', 'cell')), may hold values from 0 to 0.25
- transitions: float32 [4, 48, 48], replicated, may hold values from 0 to 1
- land_source: int32 [32768], P(('comp', 'cell')), may hold values from -1 to 127, as said below
- pair_share: float32 [32768], P(('comp', 'cell')), may hold values from 0.05 to 0.35
- river_target: int32 [32768], P(('comp', 'cell')), may hold values from -1 to 2047, as said below
- downstream_step: int32 [65536], P(('comp', 'cell')), may hold values from 0 to 2047
- river_water: float32 [4, 65536], P(None, ('comp', 'cell')), may hold values from 0.5 to 2
- river_rates: float32 [4, 65536], P(None, ('comp', 'cell')), may hold values from 0.05 to 0.8
- capacity: float32 [65536], P(('comp', 'cell')), may hold values from 0.5 to 5
Outputs:
- new_biomass: float32 [48, 64, 4096], P(None, None, ('comp', 'cell'))
- flooded: float32 [4096], P(('comp', 'cell'))
- river_state: float32 [4, 65536], P(None, ('comp', 'cell'))
Inputs may be any that keep to these rules, and one draw needn't show every extreme that they name: `land_source`: A device's list has one block of 32 rows for each receiving device, in comp+cell order; live rows come first in every block, padding rows hold -1. Every device has at least one full block, and one receiving device gets full blocks from every device. `river_target`: row s of block i on device j is live exactly when row s of block j on device i of land_source is live, and then names the receiving river cell of device j; padding rows hold -1.
All inputs are finite; a program needn't handle non-finite values.
Results may differ from a plain program's by a relative error of at most 0.0001.
Values sent between devices are 32-bit elements; how exact they have to be, the bound alone decides.
No kernel may reach another device: no remote copies, remote signals or barrier semaphores. Data moves between devices by JAX's collectives and lax.ppermute only.
A program may use at most 64 MiB of HBM per device.

v0:
```python
import jax
import jax.numpy as jnp
from jax import lax
from jax.sharding import PartitionSpec as P

NSUB = 12


highest = lax.Precision.HIGHEST


def from_behind(value, axis, steps):
    count = lax.axis_size(axis)
    initial, last = (max(0, -steps), min(count, count - steps))
    return lax.ppermute(value, axis, [(source, source + steps) for source in range(initial, last)])


def canopy(biomass, patch_area, cohort_traits, cell_forcing):
    leaf_area = biomass * cohort_traits[0][None, :, None]
    bin_count = biomass.shape[1]
    taller_mask = (jnp.arange(bin_count)[None, :] > jnp.arange(bin_count)[:, None]).astype(
        jnp.float32
    )
    leaf_above = jnp.einsum("kj,pjc->pkc", taller_mask, leaf_area, precision=highest)
    light_level = cell_forcing[0]
    assimilation = (
        cohort_traits[1][None, :, None]
        * leaf_area
        * jnp.exp(-0.05 * leaf_above)
        * (light_level / (light_level + 0.5))[None, None, :]
    )
    transpiration = 0.5 * jnp.sum(patch_area * jnp.sum(assimilation, axis=1), axis=0)
    wet_rain = cell_forcing[1] * cell_forcing[2]
    runoff = jnp.stack(
        [
            wet_rain * (1.0 - cell_forcing[4]),
            wet_rain * cell_forcing[4],
            cell_forcing[3] * jnp.exp(-0.5 * transpiration),
        ]
    )
    grown_mass = biomass * (1.0 - 0.1 * cohort_traits[2])[None, :, None] + 0.5 * assimilation
    return (grown_mass, runoff)


def transit(grown_mass, disturb_weight, transitions):
    patches, bin_count, cell_count = grown_mass.shape
    flat_mass = grown_mass.reshape(patches, bin_count * cell_count)
    transited = jnp.zeros_like(grown_mass)
    for kind_index in range(transitions.shape[0]):
        moved_mass = jnp.dot(
            transitions[kind_index],
            flat_mass,
            precision=highest,
            preferred_element_type=jnp.float32,
        )
        transited = (
            transited
            + moved_mass.reshape(patches, bin_count, cell_count)
            * disturb_weight[kind_index][None, None, :]
        )
    return transited


def scatter_pair(outflow, slots, segments):
    return jax.ops.segment_sum(outflow.T, slots, num_segments=segments).T


def shards(
    biomass,
    patch_area,
    cohort_traits,
    cell_forcing,
    disturb_weight,
    transitions,
    land_source,
    pair_share,
    river_target,
    downstream_step,
    river_water,
    river_rates,
    capacity,
):
    land_cells = biomass.shape[2]
    rivers = river_water.shape[1]
    grown_mass, runoff = canopy(biomass, patch_area, cohort_traits, cell_forcing)
    is_live = land_source >= 0
    safe_source = jnp.where(is_live, land_source, 0)
    pair_values = jnp.where(
        is_live[None, :], pair_share[None, :] * jnp.take(runoff, safe_source, axis=1), 0.0
    )
    arrived = lax.all_to_all(pair_values, ("comp", "cell"), split_axis=1, concat_axis=1, tiled=True)
    transited = transit(grown_mass, disturb_weight, transitions)
    has_target = river_target >= 0
    safe_target = jnp.where(has_target, river_target, rivers)
    runoff_in = jax.ops.segment_sum(arrived.T, safe_target, num_segments=rivers + 1)[:rivers].T
    local_cell = jnp.arange(rivers, dtype=jnp.int32)
    down_slot = jnp.where(downstream_step > 0, local_cell + downstream_step, 2 * rivers)
    fraction = 1.0 / NSUB
    surface_in = fraction * runoff_in[0:2]
    deep_in = jnp.stack([fraction * runoff_in[2], jnp.zeros_like(runoff_in[2])])
    hill_rate = river_rates[0:2]
    channel_rate = river_rates[2:4]

    def substep(sub_index, state_pair):
        hill_water, channel = state_pair
        hill_out = hill_rate * hill_water
        outflow = channel_rate * channel
        spread = scatter_pair(outflow, down_slot, 2 * rivers + 1)
        from_above = from_behind(spread[:, rivers : 2 * rivers], ("comp", "cell"), 1)
        inflow = spread[:, :rivers] + from_above
        return (hill_water - hill_out + surface_in, channel - outflow + hill_out + inflow + deep_in)

    hill_water, channel = lax.fori_loop(0, NSUB, substep, (river_water[0:2], river_water[2:4]))
    stored_total = channel[0] + channel[1]
    inundation = stored_total / (stored_total + capacity)
    flood_back = jnp.where(has_target, inundation[jnp.where(has_target, river_target, 0)], 0.0)
    returned = lax.all_to_all(flood_back, ("comp", "cell"), split_axis=0, concat_axis=0, tiled=True)
    flooded = jax.ops.segment_sum(
        pair_share * returned,
        jnp.where(is_live, land_source, land_cells),
        num_segments=land_cells + 1,
    )[:land_cells]
    new_biomass = transited * jnp.exp(-cohort_traits[3][None, :, None] * flooded[None, None, :])
    river_state = jnp.concatenate([hill_water, channel], axis=0)
    return (new_biomass, flooded, river_state)


def solution(mesh):
    return jax.shard_map(
        shards,
        mesh=mesh,
        in_specs=(
            P(None, None, ("comp", "cell")),
            P(None, ("comp", "cell")),
            P(),
            P(None, ("comp", "cell")),
            P(None, ("comp", "cell")),
            P(),
            P(("comp", "cell")),
            P(("comp", "cell")),
            P(("comp", "cell")),
            P(("comp", "cell")),
            P(None, ("comp", "cell")),
            P(None, ("comp", "cell")),
            P(("comp", "cell")),
        ),
        out_specs=(P(None, None, ("comp", "cell")), P(("comp", "cell")), P(None, ("comp", "cell"))),
        check_vma=False,
    )
```

profile of v0, /device:TPU:0, one launch (start us, length us, event | category | flops | bytes accessed | tf_op | source)
XLA Modules:
  0.0 387.7 jit_solution(3660784796597169352)
XLA Ops:
  3.6 3.6 fusion.52
  11.4 7.5 %all-to-all-start = ((f32[3,32,32]{2,0,1:T(4,128)}), f32[3,32,32]{2,0,1:T(4,128)S(1)}, u32[]{:S(2)}, u32[]{:S(2)}) async-start(f32[3,32,32]{2,0,1:T(4,128)} %multiply_select_fusion), calls=%async_computation | async-start | bytes 131072 | tf_op jit(solution)/shard_map/all_to_all | solution.py:91
  18.9 3.6 fusion.18
  22.5 3.6 fusion.21
  28.8 3.6 fusion.27
  45.0 6.6 %scatter_custom_fusion.1 = f32[2049,3]{1,0:T(8,128)S(1)} fusion(s32[1024]{0:T(1024)S(1)} %get-tuple-element.76, f32[1024,3]{1,0:T(8,128)S(1)} %copy.67, f32[]{:T(128)} %constant.23.clone.1), kind=kCustom, calls=%fused_computation.45 | custom fusion | flops 3072 | bytes 24592 | tf_op jit(solution)/shard_map/scatter-add | solution.py:95
  54.2 300.7 %while.12 = (s32[]{:T(128)}, f32[2,2048]{0,1:T(8,128)}, f32[2,2048]{0,1:T(8,128)S(1)}, f32[2,2048]{0,1:T(8,128)}, f32[2,2048]{0,1:T(8,128)}, /*index=5*/f32[2,20...) while((s32[]{:T(128)}, f32[2,2048]{0,1:T(8,128)}, f32[2,2048]{0,1:T(8,128)S(1)}, ...), condition=%wide.region_5.6_spmd, body=%wide.region_3.5_spmd.sunk | while | flops 45058 | bytes 1851629 | solution.py:113
  54.2 12.4 %scatter_custom_fusion.9 = f32[4097,2]{1,0:T(8,128)S(1)} fusion(s32[2048]{0:T(1024)S(1)} %get-tuple-element.177, f32[]{:T(128)} %constant.23.clone.1..sunk, f32[2,2048]{0,1:T(8,128)} %get-tuple-element.176, f32[2,2048]{0,1:T(8,128)S(1)} %get-tuple-element.163), kind=kCustom, calls=%fused_computation.5.clone.1 | custom fusion | flops 8192 | bytes 1097740 | tf_op jit(solution)/shard_map/while/body/eval_jaxpr/scatter-add | solution.py:65
  71.9 3.4 subtract_add_fusion.2
  78.7 12.4 %scatter_custom_fusion.9 = f32[4097,2]{1,0:T(8,128)S(1)} fusion(s32[2048]{0:T(1024)S(1)} %get-tuple-element.177, f32[]{:T(128)} %constant.23.clone.1..sunk, f32[2,2048]{0,1:T(8,128)} %get-tuple-element.176, f32[2,2048]{0,1:T(8,128)S(1)} %get-tuple-element.163), kind=kCustom, calls=%fused_computation.5.clone.1 | custom fusion | flops 8192 | bytes 1097740 | tf_op jit(solution)/shard_map/while/body/eval_jaxpr/scatter-add | solution.py:65
  94.2 3.5 collective-permute-start
  104.5 12.4 %scatter_custom_fusion.9 = f32[4097,2]{1,0:T(8,128)S(1)} fusion(s32[2048]{0:T(1024)S(1)} %get-tuple-element.177, f32[]{:T(128)} %constant.23.clone.1..sunk, f32[2,2048]{0,1:T(8,128)} %get-tuple-element.176, f32[2,2048]{0,1:T(8,128)S(1)} %get-tuple-element.163), kind=kCustom, calls=%fused_computation.5.clone.1 | custom fusion | flops 8192 | bytes 1097740 | tf_op jit(solution)/shard_map/while/body/eval_jaxpr/scatter-add | solution.py:65
  122.0 3.4 subtract_add_fusion.2
  128.8 12.4 %scatter_custom_fusion.9 = f32[4097,2]{1,0:T(8,128)S(1)} fusion(s32[2048]{0:T(1024)S(1)} %get-tuple-element.177, f32[]{:T(128)} %constant.23.clone.1..sunk, f32[2,2048]{0,1:T(8,128)} %get-tuple-element.176, f32[2,2048]{0,1:T(8,128)S(1)} %get-tuple-element.163), kind=kCustom, calls=%fused_computation.5.clone.1 | custom fusion | flops 8192 | bytes 1097740 | tf_op jit(solution)/shard_map/while/body/eval_jaxpr/scatter-add | solution.py:65
  144.4 3.5 collective-permute-start
  147.8 3.4 subtract_add_fusion.2
  154.6 12.4 %scatter_custom_fusion.9 = f32[4097,2]{1,0:T(8,128)S(1)} fusion(s32[2048]{0:T(1024)S(1)} %get-tuple-element.177, f32[]{:T(128)} %constant.23.clone.1..sunk, f32[2,2048]{0,1:T(8,128)} %get-tuple-element.176, f32[2,2048]{0,1:T(8,128)S(1)} %get-tuple-element.163), kind=kCustom, calls=%fused_computation.5.clone.1 | custom fusion | flops 8192 | bytes 1097740 | tf_op jit(solution)/shard_map/while/body/eval_jaxpr/scatter-add | solution.py:65
  179.0 12.4 %scatter_custom_fusion.9 = f32[4097,2]{1,0:T(8,128)S(1)} fusion(s32[2048]{0:T(1024)S(1)} %get-tuple-element.177, f32[]{:T(128)} %constant.23.clone.1..sunk, f32[2,2048]{0,1:T(8,128)} %get-tuple-element.176, f32[2,2048]{0,1:T(8,128)S(1)} %get-tuple-element.163), kind=kCustom, calls=%fused_computation.5.clone.1 | custom fusion | flops 8192 | bytes 1097740 | tf_op jit(solution)/shard_map/while/body/eval_jaxpr/scatter-add | solution.py:65
  194.5 3.5 collective-permute-start
  204.8 12.4 %scatter_custom_fusion.9 = f32[4097,2]{1,0:T(8,128)S(1)} fusion(s32[2048]{0:T(1024)S(1)} %get-tuple-element.177, f32[]{:T(128)} %constant.23.clone.1..sunk, f32[2,2048]{0,1:T(8,128)} %get-tuple-element.176, f32[2,2048]{0,1:T(8,128)S(1)} %get-tuple-element.163), kind=kCustom, calls=%fused_computation.5.clone.1 | custom fusion | flops 8192 | bytes 1097740 | tf_op jit(solution)/shard_map/while/body/eval_jaxpr/scatter-add | solution.py:65
  222.3 3.4 subtract_add_fusion.2
  229.1 12.4 %scatter_custom_fusion.9 = f32[4097,2]{1,0:T(8,128)S(1)} fusion(s32[2048]{0:T(1024)S(1)} %get-tuple-element.177, f32[]{:T(128)} %constant.23.clone.1..sunk, f32[2,2048]{0,1:T(8,128)} %get-tuple-element.176, f32[2,2048]{0,1:T(8,128)S(1)} %get-tuple-element.163), kind=kCustom, calls=%fused_computation.5.clone.1 | custom fusion | flops 8192 | bytes 1097740 | tf_op jit(solution)/shard_map/while/body/eval_jaxpr/scatter-add | solution.py:65
  248.0 3.4 subtract_add_fusion.2
  254.8 12.4 %scatter_custom_fusion.9 = f32[4097,2]{1,0:T(8,128)S(1)} fusion(s32[2048]{0:T(1024)S(1)} %get-tuple-element.177, f32[]{:T(128)} %constant.23.clone.1..sunk, f32[2,2048]{0,1:T(8,128)} %get-tuple-element.176, f32[2,2048]{0,1:T(8,128)S(1)} %get-tuple-element.163), kind=kCustom, calls=%fused_computation.5.clone.1 | custom fusion | flops 8192 | bytes 1097740 | tf_op jit(solution)/shard_map/while/body/eval_jaxpr/scatter-add | solution.py:65
  279.2 12.4 %scatter_custom_fusion.9 = f32[4097,2]{1,0:T(8,128)S(1)} fusion(s32[2048]{0:T(1024)S(1)} %get-tuple-element.177, f32[]{:T(128)} %constant.23.clone.1..sunk, f32[2,2048]{0,1:T(8,128)} %get-tuple-element.176, f32[2,2048]{0,1:T(8,128)S(1)} %get-tuple-element.163), kind=kCustom, calls=%fused_computation.5.clone.1 | custom fusion | flops 8192 | bytes 1097740 | tf_op jit(solution)/shard_map/while/body/eval_jaxpr/scatter-add | solution.py:65
  304.9 12.4 %scatter_custom_fusion.9 = f32[4097,2]{1,0:T(8,128)S(1)} fusion(s32[2048]{0:T(1024)S(1)} %get-tuple-element.177, f32[]{:T(128)} %constant.23.clone.1..sunk, f32[2,2048]{0,1:T(8,128)} %get-tuple-element.176, f32[2,2048]{0,1:T(8,128)S(1)} %get-tuple-element.163), kind=kCustom, calls=%fused_computation.5.clone.1 | custom fusion | flops 8192 | bytes 1097740 | tf_op jit(solution)/shard_map/while/body/eval_jaxpr/scatter-add | solution.py:65
  329.2 12.4 %scatter_custom_fusion.9 = f32[4097,2]{1,0:T(8,128)S(1)} fusion(s32[2048]{0:T(1024)S(1)} %get-tuple-element.177, f32[]{:T(128)} %constant.23.clone.1..sunk, f32[2,2048]{0,1:T(8,128)} %get-tuple-element.176, f32[2,2048]{0,1:T(8,128)S(1)} %get-tuple-element.163), kind=kCustom, calls=%fused_computation.5.clone.1 | custom fusion | flops 8192 | bytes 1097740 | tf_op jit(solution)/shard_map/while/body/eval_jaxpr/scatter-add | solution.py:65
  356.5 6.2 %gather_fusion.1 = f32[1024]{0:T(1024)S(1)} fusion(f32[2048]{0:T(1024)S(1)} %add_divide_fusion, s32[1024]{0:T(1024)S(1)} %get-tuple-element.75), kind=kCustom, calls=%fused_computation.1 | custom fusion | bytes 12288 | tf_op jit(solution)/shard_map/gather | solution.py:116
  363.4 4.6 %all-to-all-start.1 = ((f32[32,32,1]{1,2,0:T(1,128)}), f32[32,32,1]{1,2,0:T(1,128)S(1)}, u32[]{:S(2)}, u32[]{:S(2)}) async-start(f32[32,32,1]{1,2,0:T(1,128)} %bitcast.26), calls=%async_computation.1 | async-start | bytes 32768 | tf_op jit(solution)/shard_map/all_to_all | solution.py:117
  368.6 6.5 %all-to-all-done.1 = f32[32,32,1]{1,2,0:T(1,128)S(1)} async-done(((f32[32,32,1]{1,2,0:T(1,128)}), f32[32,32,1]{1,2,0:T(1,128)S(1)}, u32[]{:S(2)}, u32[]{:S(2)}) %all-to-all-start.1) | async-done | bytes 4128 | tf_op jit(solution)/shard_map/all_to_all | solution.py:117
  376.4 7.6 %scatter_custom_fusion.2 = f32[129]{0:T(256)S(1)} fusion(s32[1024]{0:T(1024)S(1)} %get-tuple-element.80, f32[1024]{0:T(1024)S(1)} %mul.241, f32[]{:T(128)} %constant.23.clone.1), kind=kCustom, calls=%fused_computation.78 | custom fusion | flops 1024 | bytes 520 | tf_op jit(solution)/shard_map/scatter-add | solution.py:118
  384.1 3.6 fusion.5
  (277 shorter events, 152.2 us)
Async XLA Ops:
  3.5 3.7 copy-start.11
  3.5 3.7 copy-start.17
  3.5 7.1 %copy-start.13 = (f32[1024]{0:T(1024)S(1)}, f32[1024]{0:T(1024)}, u32[]{:S(2)}) copy-start(f32[1024]{0:T(1024)} %param.22) | copy-start | bytes 12292
  3.6 15.3 %copy-start.8 = (f32[4,48,48]{2,1,0:T(8,128)S(1)}, f32[4,48,48]{2,1,0:T(8,128)}, u32[]{:S(2)}) copy-start(f32[4,48,48]{2,1,0:T(8,128)} %param.20) | copy-start | bytes 110596
  11.4 33.3 %all-to-all-start = ((f32[3,32,32]{2,0,1:T(4,128)}), f32[3,32,32]{2,0,1:T(4,128)S(1)}, u32[]{:S(2)}, u32[]{:S(2)}) async-start(f32[3,32,32]{2,0,1:T(4,128)} %multiply_select_fusion), calls=%async_computation | async-start | bytes 131072 | tf_op jit(solution)/shard_map/all_to_all | solution.py:91
  68.1 3.8 copy-start
  69.7 8.0 %collective-permute-start = (f32[2,2048]{1,0:T(2,128)S(1)}, f32[2,2048]{1,0:T(2,128)S(1)}, u32[]{:S(2)}, u32[]{:S(2)}) collective-permute-start(f32[2,2048]{1,0:T(2,128)S(1)} %copy.103), channel_id=1, source_target_pairs={{0,1},{1,2},{2,3},{3,4},{4,5},{5,6},{6,7},{7,8},{8,9},{9,10},{10,1... | collective-permute-start | bytes 49160 | tf_op jit(solution)/shard_map/while/body/eval_jaxpr/ppermute | solution.py:15
  92.6 5.2 %copy-start = (f32[2,2048]{0,1:T(8,128)S(1)}, f32[2,2048]{0,1:T(8,128)}, u32[]{:S(2)}) copy-start(f32[2,2048]{0,1:T(8,128)} %get-tuple-element.176) | copy-start | bytes 49156 | tf_op jit(solution)/shard_map/while
  94.2 9.3 %collective-permute-start = (f32[2,2048]{1,0:T(2,128)S(1)}, f32[2,2048]{1,0:T(2,128)S(1)}, u32[]{:S(2)}, u32[]{:S(2)}) collective-permute-start(f32[2,2048]{1,0:T(2,128)S(1)} %copy.103), channel_id=1, source_target_pairs={{0,1},{1,2},{2,3},{3,4},{4,5},{5,6},{6,7},{7,8},{8,9},{9,10},{10,1... | collective-permute-start | bytes 49160 | tf_op jit(solution)/shard_map/while/body/eval_jaxpr/ppermute | solution.py:15
  120.1 7.8 %collective-permute-start = (f32[2,2048]{1,0:T(2,128)S(1)}, f32[2,2048]{1,0:T(2,128)S(1)}, u32[]{:S(2)}, u32[]{:S(2)}) collective-permute-start(f32[2,2048]{1,0:T(2,128)S(1)} %copy.103), channel_id=1, source_target_pairs={{0,1},{1,2},{2,3},{3,4},{4,5},{5,6},{6,7},{7,8},{8,9},{9,10},{10,1... | collective-permute-start | bytes 49160 | tf_op jit(solution)/shard_map/while/body/eval_jaxpr/ppermute | solution.py:15
  142.7 5.1 %copy-start = (f32[2,2048]{0,1:T(8,128)S(1)}, f32[2,2048]{0,1:T(8,128)}, u32[]{:S(2)}) copy-start(f32[2,2048]{0,1:T(8,128)} %get-tuple-element.176) | copy-start | bytes 49156 | tf_op jit(solution)/shard_map/while
  144.4 9.3 %collective-permute-start = (f32[2,2048]{1,0:T(2,128)S(1)}, f32[2,2048]{1,0:T(2,128)S(1)}, u32[]{:S(2)}, u32[]{:S(2)}) collective-permute-start(f32[2,2048]{1,0:T(2,128)S(1)} %copy.103), channel_id=1, source_target_pairs={{0,1},{1,2},{2,3},{3,4},{4,5},{5,6},{6,7},{7,8},{8,9},{9,10},{10,1... | collective-permute-start | bytes 49160 | tf_op jit(solution)/shard_map/while/body/eval_jaxpr/ppermute | solution.py:15
  168.5 3.7 copy-start
  170.2 7.8 %collective-permute-start = (f32[2,2048]{1,0:T(2,128)S(1)}, f32[2,2048]{1,0:T(2,128)S(1)}, u32[]{:S(2)}, u32[]{:S(2)}) collective-permute-start(f32[2,2048]{1,0:T(2,128)S(1)} %copy.103), channel_id=1, source_target_pairs={{0,1},{1,2},{2,3},{3,4},{4,5},{5,6},{6,7},{7,8},{8,9},{9,10},{10,1... | collective-permute-start | bytes 49160 | tf_op jit(solution)/shard_map/while/body/eval_jaxpr/ppermute | solution.py:15
  192.9 5.1 %copy-start = (f32[2,2048]{0,1:T(8,128)S(1)}, f32[2,2048]{0,1:T(8,128)}, u32[]{:S(2)}) copy-start(f32[2,2048]{0,1:T(8,128)} %get-tuple-element.176) | copy-start | bytes 49156 | tf_op jit(solution)/shard_map/while
  194.5 9.3 %collective-permute-start = (f32[2,2048]{1,0:T(2,128)S(1)}, f32[2,2048]{1,0:T(2,128)S(1)}, u32[]{:S(2)}, u32[]{:S(2)}) collective-permute-start(f32[2,2048]{1,0:T(2,128)S(1)} %copy.103), channel_id=1, source_target_pairs={{0,1},{1,2},{2,3},{3,4},{4,5},{5,6},{6,7},{7,8},{8,9},{9,10},{10,1... | collective-permute-start | bytes 49160 | tf_op jit(solution)/shard_map/while/body/eval_jaxpr/ppermute | solution.py:15
  218.7 3.6 copy-start
  220.3 7.8 %collective-permute-start = (f32[2,2048]{1,0:T(2,128)S(1)}, f32[2,2048]{1,0:T(2,128)S(1)}, u32[]{:S(2)}, u32[]{:S(2)}) collective-permute-start(f32[2,2048]{1,0:T(2,128)S(1)} %copy.103), channel_id=1, source_target_pairs={{0,1},{1,2},{2,3},{3,4},{4,5},{5,6},{6,7},{7,8},{8,9},{9,10},{10,1... | collective-permute-start | bytes 49160 | tf_op jit(solution)/shard_map/while/body/eval_jaxpr/ppermute | solution.py:15
  243.0 5.0 %copy-start = (f32[2,2048]{0,1:T(8,128)S(1)}, f32[2,2048]{0,1:T(8,128)}, u32[]{:S(2)}) copy-start(f32[2,2048]{0,1:T(8,128)} %get-tuple-element.176) | copy-start | bytes 49156 | tf_op jit(solution)/shard_map/while
  244.6 9.2 %collective-permute-start = (f32[2,2048]{1,0:T(2,128)S(1)}, f32[2,2048]{1,0:T(2,128)S(1)}, u32[]{:S(2)}, u32[]{:S(2)}) collective-permute-start(f32[2,2048]{1,0:T(2,128)S(1)} %copy.103), channel_id=1, source_target_pairs={{0,1},{1,2},{2,3},{3,4},{4,5},{5,6},{6,7},{7,8},{8,9},{9,10},{10,1... | collective-permute-start | bytes 49160 | tf_op jit(solution)/shard_map/while/body/eval_jaxpr/ppermute | solution.py:15
  268.7 3.7 copy-start
  270.3 7.8 %collective-permute-start = (f32[2,2048]{1,0:T(2,128)S(1)}, f32[2,2048]{1,0:T(2,128)S(1)}, u32[]{:S(2)}, u32[]{:S(2)}) collective-permute-start(f32[2,2048]{1,0:T(2,128)S(1)} %copy.103), channel_id=1, source_target_pairs={{0,1},{1,2},{2,3},{3,4},{4,5},{5,6},{6,7},{7,8},{8,9},{9,10},{10,1... | collective-permute-start | bytes 49160 | tf_op jit(solution)/shard_map/while/body/eval_jaxpr/ppermute | solution.py:15
  293.1 5.0 %copy-start = (f32[2,2048]{0,1:T(8,128)S(1)}, f32[2,2048]{0,1:T(8,128)}, u32[]{:S(2)}) copy-start(f32[2,2048]{0,1:T(8,128)} %get-tuple-element.176) | copy-start | bytes 49156 | tf_op jit(solution)/shard_map/while
  294.7 9.2 %collective-permute-start = (f32[2,2048]{1,0:T(2,128)S(1)}, f32[2,2048]{1,0:T(2,128)S(1)}, u32[]{:S(2)}, u32[]{:S(2)}) collective-permute-start(f32[2,2048]{1,0:T(2,128)S(1)} %copy.103), channel_id=1, source_target_pairs={{0,1},{1,2},{2,3},{3,4},{4,5},{5,6},{6,7},{7,8},{8,9},{9,10},{10,1... | collective-permute-start | bytes 49160 | tf_op jit(solution)/shard_map/while/body/eval_jaxpr/ppermute | solution.py:15
  318.8 3.7 copy-start
  320.4 7.8 %collective-permute-start = (f32[2,2048]{1,0:T(2,128)S(1)}, f32[2,2048]{1,0:T(2,128)S(1)}, u32[]{:S(2)}, u32[]{:S(2)}) collective-permute-start(f32[2,2048]{1,0:T(2,128)S(1)} %copy.103), channel_id=1, source_target_pairs={{0,1},{1,2},{2,3},{3,4},{4,5},{5,6},{6,7},{7,8},{8,9},{9,10},{10,1... | collective-permute-start | bytes 49160 | tf_op jit(solution)/shard_map/while/body/eval_jaxpr/ppermute | solution.py:15
  343.1 5.0 %copy-start = (f32[2,2048]{0,1:T(8,128)S(1)}, f32[2,2048]{0,1:T(8,128)}, u32[]{:S(2)}) copy-start(f32[2,2048]{0,1:T(8,128)} %get-tuple-element.176) | copy-start | bytes 49156 | tf_op jit(solution)/shard_map/while
  344.8 9.2 %collective-permute-start = (f32[2,2048]{1,0:T(2,128)S(1)}, f32[2,2048]{1,0:T(2,128)S(1)}, u32[]{:S(2)}, u32[]{:S(2)}) collective-permute-start(f32[2,2048]{1,0:T(2,128)S(1)} %copy.103), channel_id=1, source_target_pairs={{0,1},{1,2},{2,3},{3,4},{4,5},{5,6},{6,7},{7,8},{8,9},{9,10},{10,1... | collective-permute-start | bytes 49160 | tf_op jit(solution)/shard_map/while/body/eval_jaxpr/ppermute | solution.py:15
  356.5 27.6 %copy-start.6 = (f32[6,8,64,128]{3,2,1,0:T(8,128)S(1)}, f32[6,8,64,128]{3,2,1,0:T(8,128)}, u32[]{:S(2)}) copy-start(f32[6,8,64,128]{3,2,1,0:T(8,128)} %copy.77) | copy-start | bytes 4718596
  356.5 27.6 %copy-start.7 = (f32[6,8,64,128]{3,2,1,0:T(8,128)S(1)}, f32[6,8,64,128]{3,2,1,0:T(8,128)}, u32[]{:S(2)}) copy-start(f32[6,8,64,128]{3,2,1,0:T(8,128)} %copy.78) | copy-start | bytes 4718596
  363.4 11.7 %all-to-all-start.1 = ((f32[32,32,1]{1,2,0:T(1,128)}), f32[32,32,1]{1,2,0:T(1,128)S(1)}, u32[]{:S(2)}, u32[]{:S(2)}) async-start(f32[32,32,1]{1,2,0:T(1,128)} %bitcast.26), calls=%async_computation.1 | async-start | bytes 32768 | tf_op jit(solution)/shard_map/all_to_all | solution.py:117
  384.0 3.7 copy-start.18
  (34 other events, 62.5 us)
where the time goes:
time: 390 us; the launch traced here: 388 us
  other arithmetic  217 us (56%)
  local copies, waits for them, and re-layouts  101 us (26%)
  starting transfers between devices  44.8 us (11%)
  matrix products  17.1 us (4%)
  waiting for transfers between devices  6.5 us (2%)
    scatter-add x12, other arithmetic, scatter_pair(): return jax.ops.segment_sum(outflow.T, slots, num_segments=segments).T  149 us
    add x12, other arithmetic, substep(): hill_water - hill_out + surface_in  41.4 us
    slice x24, local copies, waits for them, and re-layouts, substep(): from_above = from_behind(spread[:, rivers:2 * rivers], ('comp', 'cell'), 1)  37.1 us
    ppermute x12, starting transfers between devices, from_behind(): lax.ppermute(value, axis, [(source, source + steps) for source in range(i...  32.7 us
    sub x12, local copies, waits for them, and re-layouts, substep(): channel - outflow + hill_out + inflow + deep_in  19.7 us
    dot_general x4, matrix products, transit(): jnp.dot(transitions[kind_index], flat_mass, precision=highest, preferred_...  13.4 us
    unnamed x40, local copies, waits for them, and re-layouts  12.5 us
  transfers between devices with their start and end apart: 14, of which 1 were waited for; matrix products, arithmetic and copies ran while one was open for 25% of the time, Pallas kernels for 0%

commit v1 on v0

v1 whole, which is shorter than its diff:
```python
import functools
import math

import jax
import jax.numpy as jnp
from jax import lax
from jax.experimental import pallas as pl
from jax.experimental.pallas import tpu as pltpu
from jax.sharding import PartitionSpec as P

NSUB = 12
LANES = 128
GROUP = 4
F32 = jnp.float32
BF16 = jnp.bfloat16

VMEM = pl.BlockSpec(memory_space=pltpu.VMEM)
SMEM = pl.BlockSpec(memory_space=pltpu.SMEM)


def lane_iota(shape):
    return lax.broadcasted_iota(jnp.int32, shape, len(shape) - 1)


def row_iota(shape):
    return lax.broadcasted_iota(jnp.int32, shape, 0)


def nt_dot(a, b):
    return lax.dot_general(a, b, (((1,), (1,)), ((), ())), preferred_element_type=F32)


def split2(x):
    high = x.astype(BF16).astype(F32)
    return high, x - high


def by_peer(ref, peers, slots):
    rows = ref.shape[0]
    per = peers // rows
    value = ref[...]
    spread = jnp.concatenate(
        [jnp.broadcast_to(value[a : a + 1, :], (per, LANES)) for a in range(rows)], axis=0
    )
    shape = (peers, LANES)
    index = (row_iota(shape) % per) * slots + lane_iota(shape) % slots
    return jnp.take_along_axis(spread, index, axis=1, mode="promise_in_bounds")


def from_peers(ref, rows, slots, feature=None):
    peers = ref.shape[0]
    per = peers // rows
    section = lane_iota((rows, LANES)) // slots
    out = jnp.zeros((rows, LANES), F32)
    for b in range(per):
        part = ref[pl.ds(b, rows, stride=per), :]
        if feature is not None:
            shift = ((b - feature) * slots) % LANES
            if shift:
                part = pltpu.roll(part, shift, 1)
        out = jnp.where(section == b, part, out)
    return out


def statics_kernel(step_ref, rate_ref, out_ref):
    chunks = step_ref.shape[0]
    shape = (chunks, LANES)
    step = step_ref[...]
    cell = row_iota(shape) * LANES + lane_iota(shape)
    target = jnp.where(step > 0, cell + step, -1).astype(F32)
    peers = out_ref.shape[0]
    rates = []
    for q in range(2):
        row = rate_ref[2 + q : 3 + q, :]
        rates.append(
            jnp.concatenate([row[:, h * LANES : (h + 1) * LANES] for h in range(chunks)], axis=0)
        )

    def body(j, carry):
        out_ref[j, 0] = target
        out_ref[j, 1] = rates[0]
        out_ref[j, 2] = rates[1]
        return carry

    lax.fori_loop(0, peers, body, 0)


def rain_kernel(bins, slots, trait_ref, bio_ref, area_ref, force_ref, source_ref, share_ref, out_ref, total_ref):
    step = pl.program_id(0)
    patches = area_ref.shape[0]
    light = force_ref[0:1, :]
    light = light / (light + 0.5)

    @pl.when(step == 0)
    def _():
        total_ref[...] = jnp.zeros_like(total_ref)

    above = jnp.zeros((patches, LANES), F32)
    total = jnp.zeros((patches, LANES), F32)
    for k in reversed(range(bins)):
        leaf = bio_ref[pl.ds(k, patches, stride=bins), :] * trait_ref[0, k]
        total = total + trait_ref[1, k] * leaf * jnp.exp(-0.05 * above)
        above = above + leaf
    total_ref[...] += jnp.sum(total * light * area_ref[...], axis=0, keepdims=True)

    @pl.when(step == pl.num_programs(0) - 1)
    def _():
        peers = out_ref.shape[0]
        shape = (peers, LANES)
        wet = force_ref[1:2, :] * force_ref[2:3, :]
        frozen = force_ref[4:5, :]
        runoff = [
            wet * (1.0 - frozen),
            wet * frozen,
            force_ref[3:4, :] * jnp.exp(-0.5 * (0.5 * total_ref[...])),
        ]
        source = by_peer(source_ref, peers, slots)
        share = by_peer(share_ref, peers, slots)
        safe = jnp.maximum(source, 0)
        section = lane_iota(shape) // slots
        value = jnp.zeros(shape, F32)
        for f in range(3):
            taken = jnp.take_along_axis(
                jnp.broadcast_to(runoff[f], shape), safe, axis=1, mode="promise_in_bounds"
            )
            value = jnp.where(section == f, taken, value)
        out_ref[...] = jnp.where(source >= 0, share * value, 0.0)


def transit_kernel(kinds, bins, trait_ref, trans_ref, bio_ref, force_ref, weight_ref, out_ref, left_ref):
    patches = trans_ref.shape[1]
    rows = kinds * patches
    high, low = split2(trans_ref[...])
    left_ref[:, 0:patches] = high.astype(BF16)
    left_ref[:, patches : 2 * patches] = high.astype(BF16)
    left_ref[:, 2 * patches : 3 * patches] = low.astype(BF16)
    light = force_ref[0:1, :]
    light = light / (light + 0.5)
    weights = [jnp.broadcast_to(weight_ref[t : t + 1, :], (patches, LANES)) for t in range(kinds)]
    half = 0.5 * light

    def one(k, above):
        mass = bio_ref[pl.ds(k, patches, stride=bins), :]
        leaf = mass * trait_ref[0, k]
        gain = trait_ref[1, k] * leaf * jnp.exp(-0.05 * above) * half
        grown = mass * (1.0 - 0.1 * trait_ref[2, k]) + gain
        high, low = split2(grown)
        high = high.astype(BF16)
        return jnp.concatenate([high, low.astype(BF16), high], axis=0), above + leaf

    def body(i, above):
        k = bins - 1 - 2 * i
        first, above = one(k, above)
        second, above = one(k - 1, above)
        right = jnp.concatenate([first, second], axis=1)
        moved = jnp.dot(left_ref[...], right, preferred_element_type=F32)
        for j in range(2):
            part = moved[:, j * LANES : (j + 1) * LANES]
            total = part[0:patches] * weights[0]
            for t in range(1, kinds):
                total = total + part[t * patches : (t + 1) * patches] * weights[t]
            out_ref[pl.ds(k - j, patches, stride=bins), :] = total
        return above

    lax.fori_loop(0, bins // 2, body, jnp.zeros((patches, LANES), F32), unroll=4)


def river_kernel(
    slots,
    here_ref,
    static_ref,
    arrived_ref,
    target_ref,
    water_ref,
    rate_ref,
    out_ref,
    hill_out_ref,
    lo_ref,
    mask_ref,
    state_ref,
    speed_ref,
    value_ref,
    left_ref,
    rows_left_ref,
    rows_lo_ref,
    hill_ref,
    hill_rate_ref,
    force_ref,
):
    peers = static_ref.shape[0]
    chunks = static_ref.shape[2]
    spans = 2 * chunks
    window = state_ref.shape[0]
    here = here_ref[0]
    rows = target_ref.shape[0]

    def block_of(b):
        j = here + b
        return jnp.where(j >= peers, j - peers, j)

    def table(b, carry):
        j = block_of(b)
        target = static_ref[j, 0].astype(jnp.int32)
        span = target >> 7
        low = target & 127
        for h in range(chunks):
            at = slice(h * LANES, (h + 1) * LANES)
            mask_ref[b, :, at] = jnp.where(
                row_iota((spans, LANES)) == span[h : h + 1, :], 1.0, 0.0
            ).astype(BF16)
            lo_ref[b, :, at] = jnp.where(
                row_iota((LANES, LANES)) == low[h : h + 1, :], 1.0, 0.0
            ).astype(BF16)
        speed_ref[b, 0] = static_ref[j, 1]
        speed_ref[b, 1] = static_ref[j, 2]
        return carry

    lax.fori_loop(0, window - 1, table, 0)

    target = target_ref[...]
    span = target >> 7
    low = target & 127
    values = []
    for f in range(3):
        values.append(split2(from_peers(arrived_ref, rows, slots, f)))
    for a in range(rows):
        at = slice(a * LANES, (a + 1) * LANES)
        mask = row_iota((chunks, LANES)) == span[a : a + 1, :]
        for s in range(2):
            for f in range(3):
                m = (s * 3 + f) * chunks
                rows_left_ref[m : m + chunks, at] = jnp.where(
                    mask, values[f][s][a : a + 1, :], 0.0
                ).astype(BF16)
        rows_lo_ref[:, at] = jnp.where(
            row_iota((LANES, LANES)) == low[a : a + 1, :], 1.0, 0.0
        ).astype(BF16)
    taken = nt_dot(rows_left_ref[...], rows_lo_ref[...])
    fraction = 1.0 / NSUB
    half = 3 * chunks
    for f in range(3):
        force_ref[f] = fraction * (
            taken[f * chunks : (f + 1) * chunks] + taken[half + f * chunks : half + (f + 1) * chunks]
        )

    state_ref[...] = jnp.zeros_like(state_ref)
    for q in range(2):
        for h in range(chunks):
            at = slice(h * LANES, (h + 1) * LANES)
            hill_ref[q, h : h + 1, :] = water_ref[q : q + 1, at]
            hill_rate_ref[q, h : h + 1, :] = rate_ref[q : q + 1, at]
            state_ref[0, q, h : h + 1, :] = water_ref[2 + q : 3 + q, at]

    def outflow_of(b, g):
        outs = []
        for q in range(2):
            out = speed_ref[b, q] * state_ref[b, q]
            high, lowp = split2(out)
            value_ref[g, q] = high
            value_ref[g, 2 + q] = lowp
            outs.append(out)
        for h in range(chunks):
            at = slice(h * LANES, (h + 1) * LANES)
            mask = mask_ref[b, :, at]
            for sq in range(4):
                row = jnp.broadcast_to(value_ref[g, sq, h : h + 1, :], (spans, LANES))
                left_ref[g, sq * spans : (sq + 1) * spans, at] = row.astype(BF16) * mask
        return outs

    def group_step(first):
        outs = [outflow_of(first + g, g) for g in range(GROUP)]
        flows = [nt_dot(left_ref[g], lo_ref[first + g]) for g in range(GROUP)]
        for q in range(2):
            carried = None
            for g in range(GROUP):
                flow = flows[g][q * spans : (q + 1) * spans] + flows[g][(2 + q) * spans : (3 + q) * spans]
                new = state_ref[first + g, q] - outs[g][q] + flow[0:chunks]
                if carried is not None:
                    new = new + carried
                state_ref[first + g, q] = new
                carried = flow[chunks:spans]
            state_ref[first + GROUP, q] += carried

    for phase in range(NSUB // GROUP):

        def step(t, carry):
            for group in reversed(range(phase + 1)):
                group_step(group * GROUP)
            for q in range(2):
                hill = hill_ref[q]
                gone = hill_rate_ref[q] * hill
                add = gone + force_ref[2] if q == 0 else gone
                state_ref[0, q] += add
                hill_ref[q] = hill - gone + force_ref[q]
            return carry

        lax.fori_loop(0, GROUP, step, 0)

    hill_out_ref[...] = hill_ref[...]

    def send(b, carry):
        out_ref[block_of(b)] = state_ref[b]
        return carry

    lax.fori_loop(0, window, send, 0)


def inundate_kernel(slots, window, here_ref, part_ref, capacity_ref, target_ref, hill_ref, state_ref, back_ref):
    peers = part_ref.shape[0]
    chunks = capacity_ref.shape[0]
    here = here_ref[0]
    channel = jnp.zeros(part_ref.shape[1:], F32)
    for b in range(window):
        j = here - b
        j = jnp.where(j < 0, j + peers, j)
        channel = channel + part_ref[j]
    for q in range(2):
        for h in range(chunks):
            at = slice(h * LANES, (h + 1) * LANES)
            state_ref[q : q + 1, at] = hill_ref[q, h : h + 1, :]
            state_ref[2 + q : 3 + q, at] = channel[q, h : h + 1, :]
    stored = channel[0] + channel[1]
    wet = stored / (stored + capacity_ref[...])
    target = by_peer(target_ref, peers, slots)
    span = target >> 7
    low = target & 127
    back = jnp.zeros((peers, LANES), F32)
    for h in range(chunks):
        taken = jnp.take_along_axis(
            jnp.broadcast_to(wet[h : h + 1, :], (peers, LANES)), low, axis=1, mode="promise_in_bounds"
        )
        back = jnp.where(span == h, taken, back)
    back_ref[...] = back


def survive_kernel(bins, slots, trait_ref, back_ref, share_ref, source_ref, moved_ref, out_ref, flooded_ref, alive_ref):
    @pl.when(pl.program_id(0) == 0)
    def _():
        rows = share_ref.shape[0]
        value = share_ref[...] * from_peers(back_ref, rows, slots)
        source = source_ref[...]
        total = jnp.zeros((LANES, LANES), F32)
        for a in range(rows):
            total = total + jnp.where(
                row_iota((LANES, LANES)) == source[a : a + 1, :], value[a : a + 1, :], 0.0
            )
        flooded = jnp.sum(total.T, axis=0, keepdims=True)
        flooded_ref[...] = flooded
        for k in range(bins):
            alive_ref[k : k + 1, :] = jnp.exp(-trait_ref[3, k] * flooded)

    alive = alive_ref[...]
    for p in range(moved_ref.shape[0] // bins):
        at = slice(p * bins, (p + 1) * bins)
        out_ref[at, :] = moved_ref[at, :] * alive


def shards(
    axes,
    biomass,
    patch_area,
    cohort_traits,
    cell_forcing,
    disturb_weight,
    transitions,
    land_source,
    pair_share,
    river_target,
    downstream_step,
    river_water,
    river_rates,
    capacity,
):
    patches, bins, lands = biomass.shape
    rivers = river_water.shape[1]
    peers = math.prod(lax.axis_size(a) for a in axes)
    slots = land_source.shape[0] // peers
    rows = land_source.shape[0] // LANES
    chunks = rivers // LANES
    kinds = transitions.shape[0]
    window = NSUB + 1
    here = lax.axis_index(axes).astype(jnp.int32).reshape(1)

    bio = biomass.reshape(patches * bins, lands)
    source = land_source.reshape(rows, LANES)
    share = pair_share.reshape(rows, LANES)
    target = river_target.reshape(rows, LANES)
    step = downstream_step.reshape(chunks, LANES)

    statics = pl.pallas_call(
        statics_kernel,
        out_shape=jax.ShapeDtypeStruct((peers, 3, chunks, LANES), F32),
        in_specs=[VMEM, VMEM],
        out_specs=VMEM,
        name="statics",
    )(step, river_rates)
    statics = lax.all_to_all(statics, axes, split_axis=0, concat_axis=0, tiled=True)

    tile = 16
    message = pl.pallas_call(
        functools.partial(rain_kernel, bins, slots),
        grid=(patches // tile,),
        out_shape=jax.ShapeDtypeStruct((peers, LANES), F32),
        in_specs=[
            SMEM,
            pl.BlockSpec((tile * bins, LANES), lambda i: (i, 0)),
            pl.BlockSpec((tile, LANES), lambda i: (i, 0)),
            pl.BlockSpec((5, LANES), lambda i: (0, 0)),
            pl.BlockSpec((rows, LANES), lambda i: (0, 0)),
            pl.BlockSpec((rows, LANES), lambda i: (0, 0)),
        ],
        out_specs=pl.BlockSpec((peers, LANES), lambda i: (0, 0)),
        scratch_shapes=[pltpu.VMEM((1, LANES), F32)],
        name="rain",
    )(cohort_traits, bio, patch_area, cell_forcing, source, share)
    arrived = lax.all_to_all(message, axes, split_axis=0, concat_axis=0, tiled=True)

    moved = pl.pallas_call(
        functools.partial(transit_kernel, kinds, bins),
        out_shape=jax.ShapeDtypeStruct((patches * bins, LANES), F32),
        in_specs=[SMEM, VMEM, VMEM, VMEM, VMEM],
        out_specs=VMEM,
        scratch_shapes=[pltpu.VMEM((kinds * patches, 3 * patches), BF16)],
        name="transit",
    )(cohort_traits, transitions.reshape(kinds * patches, patches), bio, cell_forcing, disturb_weight)

    spans = 2 * chunks
    parts, hill = pl.pallas_call(
        functools.partial(river_kernel, slots),
        out_shape=(
            jax.ShapeDtypeStruct((peers, 2, chunks, LANES), F32),
            jax.ShapeDtypeStruct((2, chunks, LANES), F32),
        ),
        in_specs=[SMEM] + [VMEM] * 5,
        out_specs=(VMEM, VMEM),
        scratch_shapes=[
            pltpu.VMEM((window - 1, LANES, rivers), BF16),
            pltpu.VMEM((window - 1, spans, rivers), BF16),
            pltpu.VMEM((window, 2, chunks, LANES), F32),
            pltpu.VMEM((window - 1, 2, chunks, LANES), F32),
            pltpu.VMEM((GROUP, 4, chunks, LANES), F32),
            pltpu.VMEM((GROUP, 4 * spans, rivers), BF16),
            pltpu.VMEM((6 * chunks, rows * LANES), BF16),
            pltpu.VMEM((LANES, rows * LANES), BF16),
            pltpu.VMEM((2, chunks, LANES), F32),
            pltpu.VMEM((2, chunks, LANES), F32),
            pltpu.VMEM((3, chunks, LANES), F32),
        ],
        name="river",
    )(here, statics, arrived, target, river_water, river_rates)
    parts = lax.all_to_all(parts, axes, split_axis=0, concat_axis=0, tiled=True)

    river_state, back = pl.pallas_call(
        functools.partial(inundate_kernel, slots, window),
        out_shape=(
            jax.ShapeDtypeStruct((4, rivers), F32),
            jax.ShapeDtypeStruct((peers, LANES), F32),
        ),
        in_specs=[SMEM] + [VMEM] * 4,
        out_specs=(VMEM, VMEM),
        name="inundate",
    )(here, parts, capacity.reshape(chunks, LANES), target, hill)
    back = lax.all_to_all(back, axes, split_axis=0, concat_axis=0, tiled=True)

    tile = 12
    new_biomass, flooded = pl.pallas_call(
        functools.partial(survive_kernel, bins, slots),
        grid=(patches // tile,),
        out_shape=(
            jax.ShapeDtypeStruct((patches * bins, LANES), F32),
            jax.ShapeDtypeStruct((1, LANES), F32),
        ),
        in_specs=[
            SMEM,
            pl.BlockSpec((peers, LANES), lambda i: (0, 0)),
            pl.BlockSpec((rows, LANES), lambda i: (0, 0)),
            pl.BlockSpec((rows, LANES), lambda i: (0, 0)),
            pl.BlockSpec((tile * bins, LANES), lambda i: (i, 0)),
        ],
        out_specs=(
            pl.BlockSpec((tile * bins, LANES), lambda i: (i, 0)),
            pl.BlockSpec((1, LANES), lambda i: (0, 0)),
        ),
        scratch_shapes=[pltpu.VMEM((bins, LANES), F32)],
        name="survive",
    )(cohort_traits, back, share, source, moved)
    return (new_biomass.reshape(patches, bins, lands), flooded.reshape(lands), river_state)


def solution(mesh):
    axes = tuple(mesh.axis_names)
    split = P(axes)
    split1 = P(None, axes)
    return jax.shard_map(
        functools.partial(shards, axes),
        mesh=mesh,
        in_specs=(
            P(None, None, axes),
            split1,
            P(),
            split1,
            split1,
            P(),
            split,
            split,
            split,
            split,
            split1,
            split1,
            split,
        ),
        out_specs=(P(None, None, axes), split, split1),
        check_vma=False,
    )
```

time: 390 us -> 106 us (0.27)
  other arithmetic: 217 us -> 0 us
  local copies, waits for them, and re-layouts: 101 us -> 1.48 us
  Pallas kernels: 0 us -> 44.5 us
  starting transfers between devices: 44.8 us -> 12.5 us
  waiting for transfers between devices: 6.5 us -> 27.1 us
  blocking collectives: 0 us -> 19.5 us
  matrix products: 17.1 us -> 0 us
    scatter-add x14 -> x0, other arithmetic: 163 us -> none  [the longest x12 149 us: scatter_pair(): return jax.ops.segment_sum(outflow.T, slots, num_segments=segments).T]
    pallas_call x0 -> x6, Pallas kernels: none -> 44.5 us  [the longest x1 26 us: shards(): pl.pallas_call(functools.partial(river_kernel, slots), out_shape=(jax.Sha...]
    add x37 -> x0, other arithmetic: 43.6 us -> none  [the longest x12 41.4 us: substep(): hill_water - hill_out + surface_in]
    slice x39 -> x0, local copies, waits for them, and re-layouts: 41.3 us -> none  [the longest x24 37.1 us: substep(): from_above = from_behind(spread[:, rivers:2 * rivers], ('comp', 'cell'), 1)]
    ppermute x12 -> x0, starting transfers between devices: 32.7 us -> none  [from_behind(): lax.ppermute(value, axis, [(source, source + steps) for source in range(i...]
    all_to_all x2 -> x3, waiting for transfers between devices: 6.47 us -> 27.1 us  [the longest x1 21.8 us: shards(): lax.all_to_all(statics, axes, split_axis=0, concat_axis=0, tiled=True)]
    sub x12 -> x0, local copies, waits for them, and re-layouts: 19.7 us -> none  [substep(): channel - outflow + hill_out + inflow + deep_in]
    all_to_all x0 -> x1, blocking collectives: none -> 19.5 us  [shards(): parts = lax.all_to_all(parts, axes, split_axis=0, concat_axis=0, tiled=True)]
  transfers between devices with their start and end apart: 14 -> 3, of which waited for: 1 -> 2; matrix products, arithmetic and copies ran while one was open for 25% -> 0% of each run, Pallas kernels for 0% -> 9%
where the time goes in v1:
time: 106 us
  Pallas kernels  44.5 us (42%)
  waiting for transfers between devices  27.1 us (26%)
  blocking collectives  19.5 us (18%)
  starting transfers between devices  12.5 us (12%)
  local copies, waits for them, and re-layouts  1.48 us (1%)
    pallas_call x1, Pallas kernels, shards(): pl.pallas_call(functools.partial(river_kernel, slots), out_shape=(jax.Sha...  26 us
    all_to_all x1, waiting for transfers between devices, shards(): lax.all_to_all(statics, axes, split_axis=0, concat_axis=0, tiled=True)  21.8 us
    all_to_all x1, blocking collectives, shards(): parts = lax.all_to_all(parts, axes, split_axis=0, concat_axis=0, tiled=True)  19.5 us
    all_to_all x1, starting transfers between devices, shards(): lax.all_to_all(message, axes, split_axis=0, concat_axis=0, tiled=True)  7.33 us
    pallas_call x1, Pallas kernels, shards(): pl.pallas_call(functools.partial(transit_kernel, kinds, bins), out_shape=...  7.28 us
    all_to_all x1, waiting for transfers between devices, shards(): lax.all_to_all(message, axes, split_axis=0, concat_axis=0, tiled=True)  5.25 us
    pallas_call x1, Pallas kernels, shards(): pl.pallas_call(functools.partial(survive_kernel, bins, slots), grid=(patc...  3.77 us
    pallas_call x1, Pallas kernels, shards(): pl.pallas_call(functools.partial(rain_kernel, bins, slots), grid=(patches...  3.68 us
  transfers between devices with their start and end apart: 3, of which 2 were waited for; matrix products, arithmetic and copies ran while one was open for 0% of the time, Pallas kernels for 9%

profile of v1, /device:TPU:0, one launch (start us, length us, event | category | flops | bytes accessed | tf_op | source)
XLA Modules:
  0.0 105.8 jit_solution(12835396433161663603)
XLA Ops:
  0.6 3.7 %rain.1 = f32[32,128]{1,0:T(8,128)} custom-call(f32[4,64]{1,0:T(4,128)} %trait_ref.5, f32[3072,128]{1,0:T(8,128)} %bitcast.18, f32[48,128]{1,0:T(8,128)} %area_ref.1, f32[5,128]{1,0:T(8,128)} %force_ref.3, s32[8,128]{1,0:T(8,128)} %bitcast.26, f32[8,128]{1,0:T(8,128)} %bitcast.28), custom_call_target="tpu_custom_call" | custom-call | tf_op jit(solution)/shard_map/rain/pallas_call | solution.py:400
  4.3 7.3 %all-to-all-start.1 = ((f32[32,1,128]{2,1,0:T(1,128)}), f32[32,1,128]{2,1,0:T(1,128)S(1)}, u32[]{:S(2)}, u32[]{:S(2)}) async-start(f32[32,1,128]{2,1,0:T(1,128)} %bitcast.22), calls=%async_computation.1 | async-start | bytes 32768 | tf_op jit(solution)/shard_map/all_to_all | solution.py:416
  11.6 1.8 %statics.1 = f32[32,3,16,128]{3,2,1,0:T(8,128)} custom-call(s32[16,128]{1,0:T(8,128)} %bitcast.31, f32[4,2048]{1,0:T(4,128)} %rate_ref.3), custom_call_target="tpu_custom_call" | custom-call | tf_op jit(solution)/shard_map/statics/pallas_call | solution.py:390
  13.5 5.2 %all-to-all-done.1 = f32[32,1,128]{2,1,0:T(1,128)S(1)} async-done(((f32[32,1,128]{2,1,0:T(1,128)}), f32[32,1,128]{2,1,0:T(1,128)S(1)}, u32[]{:S(2)}, u32[]{:S(2)}) %all-to-all-start.1) | async-done | bytes 16416 | tf_op jit(solution)/shard_map/all_to_all | solution.py:416
  18.7 0.0 copy-start.2
  18.7 2.6 %all-to-all-start = ((f32[32,3,16,128]{3,2,1,0:T(8,128)}), f32[32,3,16,128]{3,2,1,0:T(8,128)S(1)}, u32[]{:S(2)}, u32[]{:S(2)}) async-start(f32[32,3,16,128]{3,2,1,0:T(8,128)} %statics.1), calls=%async_computation | async-start | bytes 1572864 | tf_op jit(solution)/shard_map/all_to_all | solution.py:397
  21.4 21.8 %all-to-all-done.static_ref = f32[32,3,16,128]{3,2,1,0:T(8,128)S(1)} async-done(((f32[32,3,16,128]{3,2,1,0:T(8,128)}), f32[32,3,16,128]{3,2,1,0:T(8,128)S(1)}, u32[]{:S(2)}, u32[]{:S(2)}) %all-to-all-start) | async-done | bytes 786464 | tf_op jit(solution)/shard_map/all_to_all | solution.py:397
  43.2 0.0 copy-start
  43.2 0.0 copy-done.2
  43.2 0.9 copy-done
  44.1 26.0 %river.1 = (f32[32,2,16,128]{3,2,1,0:T(8,128)}, f32[2,16,128]{2,1,0:T(8,128)}) custom-call(s32[1]{0:T(128)} %bitcast.here_ref, f32[32,3,16,128]{3,2,1,0:T(8,128)} %copy-done, f32[32,128]{1,0:T(8,128)} %bitcast.23, s32[8,128]{1,0:T(8,128)} %bitcast.24, f32[4,2048]{1,0:T(4,128)} %water_ref.1, f32[4,2048]{1,0:T(4,128)} %rate_ref.3), custom_call_target="tpu_custom_call" | custom-call | tf_op jit(solution)/shard_map/river/pallas_call | solution.py:428
  70.1 19.5 %all_to_all.32.part_ref = f32[32,2,16,128]{3,2,1,0:T(8,128)} all-to-all(f32[32,2,16,128]{3,2,1,0:T(8,128)} %get-tuple-element.9), channel_id=1, replica_groups=mesh['comp'=4,'cell'=8] {'comp','cell'}, dimensions={0} | all-to-all | bytes 1048576 | tf_op jit(solution)/shard_map/all_to_all | solution.py:451
  89.6 2.0 %inundate.1 = (f32[4,2048]{1,0:T(4,128)}, f32[32,128]{1,0:T(8,128)}) custom-call(s32[1]{0:T(128)} %bitcast.here_ref, f32[32,2,16,128]{3,2,1,0:T(8,128)} %all_to_all.32.part_ref, f32[16,128]{1,0:T(8,128)} %bitcast.32, s32[8,128]{1,0:T(8,128)} %bitcast.25, f32[2,16,128]{2,1,0:T(8,128)} %get-tuple-element.10.hill_ref), custom_call_target="tpu_custom_call" | custom-call | tf_op jit(solution)/shard_map/inundate/pallas_call | solution.py:453
  91.6 2.5 %all-to-all-start.3 = ((f32[32,1,128]{2,1,0:T(1,128)}), f32[32,1,128]{2,1,0:T(1,128)S(1)}, u32[]{:S(2)}, u32[]{:S(2)}) async-start(f32[32,1,128]{2,1,0:T(1,128)} %bitcast.30), calls=%async_computation.3 | async-start | bytes 32768 | tf_op jit(solution)/shard_map/all_to_all | solution.py:463
  94.2 7.3 %transit.1.moved_ref = f32[3072,128]{1,0:T(8,128)} custom-call(f32[4,64]{1,0:T(4,128)} %trait_ref.5, f32[192,48]{1,0:T(8,128)} %bitcast.20, f32[3072,128]{1,0:T(8,128)} %bitcast.19, f32[5,128]{1,0:T(8,128)} %force_ref.3, f32[4,128]{1,0:T(4,128)} %weight_ref.1), custom_call_target="tpu_custom_call" | custom-call | tf_op jit(solution)/shard_map/transit/pallas_call | solution.py:418
  101.4 0.0 all-to-all-done.3
  101.4 0.0 copy-start.1
  101.4 0.6 copy-done.1
  102.0 3.8 %survive.1 = (f32[3072,128]{1,0:T(8,128)}, f32[1,128]{1,0:T(1,128)}) custom-call(f32[4,64]{1,0:T(4,128)} %trait_ref.5, f32[32,128]{1,0:T(8,128)} %bitcast.21, f32[8,128]{1,0:T(8,128)} %bitcast.29, s32[8,128]{1,0:T(8,128)} %bitcast.27, f32[3072,128]{1,0:T(8,128)} %transit.1.moved_ref), custom_call_target="tpu_custom_call" | custom-call | tf_op jit(solution)/shard_map/survive/pallas_call | solution.py:466
Async XLA Ops:
  4.3 14.4 %all-to-all-start.1 = ((f32[32,1,128]{2,1,0:T(1,128)}), f32[32,1,128]{2,1,0:T(1,128)S(1)}, u32[]{:S(2)}, u32[]{:S(2)}) async-start(f32[32,1,128]{2,1,0:T(1,128)} %bitcast.22), calls=%async_computation.1 | async-start | bytes 32768 | tf_op jit(solution)/shard_map/all_to_all | solution.py:416
  18.7 24.5 %copy-start.2 = (f32[32,1,128]{2,1,0:T(1,128)}, f32[32,1,128]{2,1,0:T(1,128)S(1)}, u32[]{:S(2)}) copy-start(f32[32,1,128]{2,1,0:T(1,128)S(1)} %all-to-all-done.1) | copy-start | bytes 49156
  18.7 24.5 %all-to-all-start = ((f32[32,3,16,128]{3,2,1,0:T(8,128)}), f32[32,3,16,128]{3,2,1,0:T(8,128)S(1)}, u32[]{:S(2)}, u32[]{:S(2)}) async-start(f32[32,3,16,128]{3,2,1,0:T(8,128)} %statics.1), calls=%async_computation | async-start | bytes 1572864 | tf_op jit(solution)/shard_map/all_to_all | solution.py:397
  43.2 0.9 copy-start
  91.6 9.8 %all-to-all-start.3 = ((f32[32,1,128]{2,1,0:T(1,128)}), f32[32,1,128]{2,1,0:T(1,128)S(1)}, u32[]{:S(2)}, u32[]{:S(2)}) async-start(f32[32,1,128]{2,1,0:T(1,128)} %bitcast.30), calls=%async_computation.3 | async-start | bytes 32768 | tf_op jit(solution)/shard_map/all_to_all | solution.py:463
  101.4 0.6 copy-start.1

commit v2 on v1

v2 whole, which is shorter than its diff:
```python
import functools
import math

import jax
import jax.numpy as jnp
from jax import lax
from jax.experimental import pallas as pl
from jax.experimental.pallas import tpu as pltpu
from jax.sharding import PartitionSpec as P


NSUB = 12
LANES = 128
PHASE = 2
F32 = jnp.float32
BF16 = jnp.bfloat16

VMEM = pl.BlockSpec(memory_space=pltpu.VMEM)
ANY = pl.BlockSpec(memory_space=pl.ANY)
SMEM = pl.BlockSpec(memory_space=pltpu.SMEM)


def lane_iota(shape):
    return lax.broadcasted_iota(jnp.int32, shape, len(shape) - 1)


def row_iota(shape):
    return lax.broadcasted_iota(jnp.int32, shape, 0)


def nt_dot(a, b):
    return lax.dot_general(a, b, (((1,), (1,)), ((), ())), preferred_element_type=F32)


def split2(x):
    high = x.astype(BF16).astype(F32)
    return high, x - high


def by_peer(ref, peers, slots):
    rows = ref.shape[0]
    per = peers // rows
    value = ref[...]
    spread = jnp.concatenate(
        [jnp.broadcast_to(value[a : a + 1, :], (per, LANES)) for a in range(rows)], axis=0
    )
    shape = (peers, LANES)
    index = (row_iota(shape) % per) * slots + lane_iota(shape) % slots
    return jnp.take_along_axis(spread, index, axis=1, mode="promise_in_bounds")


def from_peers(ref, rows, slots, feature=None, which=0, count=1):
    peers = ref.shape[0] // count
    per = peers // rows
    section = lane_iota((rows, LANES)) // slots
    out = jnp.zeros((rows, LANES), F32)
    for b in range(per):
        part = ref[pl.ds(b * count + which, rows, stride=per * count), :]
        if feature is not None:
            shift = ((b - feature) * slots) % LANES
            if shift:
                part = pltpu.roll(part, shift, 1)
        out = jnp.where(section == b, part, out)
    return out


def unrow(row, chunks):
    return jnp.concatenate([row[:, h * LANES : (h + 1) * LANES] for h in range(chunks)], axis=0)


def rain_kernel(
    bins,
    slots,
    core_ref,
    trait_ref,
    bio_ref,
    area_ref,
    force_ref,
    source_ref,
    share_ref,
    step_ref,
    target_ref,
    water_ref,
    rate_ref,
    out_ref,
    mate_ref,
    total_ref,
    static_ref,
    rows_ref,
    sems,
    rows_sem,
):
    step = pl.program_id(0)
    patches = area_ref.shape[0]
    peers = out_ref.shape[0]
    chunks = step_ref.shape[0]
    light = force_ref[0:1, :]
    light = light / (light + 0.5)

    def spread(j):
        return pltpu.make_async_copy(
            static_ref.at[j % 2], out_ref.at[j, pl.ds(0, 2 * chunks)], sems.at[j]
        )

    @pl.when(step == 0)
    def _():
        total_ref[...] = jnp.zeros_like(total_ref)
        shape = (chunks, LANES)
        moves = step_ref[...]
        cell = row_iota(shape) * LANES + lane_iota(shape)
        target = jnp.where(moves > 0, cell + moves, -1).astype(F32)
        for q in range(2):
            static_ref[q, 0:chunks, :] = target
            static_ref[q, chunks : 2 * chunks, :] = unrow(rate_ref[2 + q : 3 + q, :], chunks)
        for j in range(peers):
            spread(j).start()
        first = core_ref[0] == 0
        for i, (ref, at) in enumerate(((water_ref, 2), (water_ref, 0), (rate_ref, 0))):
            other = jnp.where(first, ref[at + 1 : at + 2, :], ref[at : at + 1, :])
            mate_ref[i * chunks : (i + 1) * chunks, :] = unrow(other, chunks)
        mate_ref[3 * chunks :, :] = target_ref[...].astype(F32)

    above = jnp.zeros((patches, LANES), F32)
    total = jnp.zeros((patches, LANES), F32)
    for k in reversed(range(bins)):
        leaf = bio_ref[pl.ds(k, patches, stride=bins), :] * trait_ref[0, k]
        total = total + trait_ref[1, k] * leaf * jnp.exp(-0.05 * above)
        above = above + leaf
    total_ref[...] += jnp.sum(total * light * area_ref[...], axis=0, keepdims=True)

    @pl.when(step == pl.num_programs(0) - 1)
    def _():
        shape = (peers, LANES)
        wet = force_ref[1:2, :] * force_ref[2:3, :]
        frozen = force_ref[4:5, :]
        runoff = [
            wet * (1.0 - frozen),
            wet * frozen,
            force_ref[3:4, :] * jnp.exp(-0.5 * (0.5 * total_ref[...])),
        ]
        source = by_peer(source_ref, peers, slots)
        share = by_peer(share_ref, peers, slots)
        safe = jnp.maximum(source, 0)
        section = lane_iota(shape) // slots
        value = jnp.zeros(shape, F32)
        for f in range(3):
            taken = jnp.take_along_axis(
                jnp.broadcast_to(runoff[f], shape), safe, axis=1, mode="promise_in_bounds"
            )
            value = jnp.where(section == f, taken, value)
        own = jnp.where(source >= 0, share * value, 0.0)
        mate = jnp.where(
            row_iota(shape) % 2 == 0, pltpu.roll(own, peers - 1, 0), pltpu.roll(own, 1, 0)
        )
        rows_ref[pl.ds(0, peers, stride=8), :] = own
        rows_ref[pl.ds(1, peers, stride=8), :] = mate
        copy = pltpu.make_async_copy(
            rows_ref.reshape(peers, 8, LANES), out_ref.at[:, pl.ds(2 * chunks, 8)], rows_sem
        )
        copy.start()
        for j in range(peers):
            spread(j).wait()
        copy.wait()


def transit_kernel(kinds, bins, trait_ref, trans_ref, bio_ref, force_ref, weight_ref, out_ref, left_ref):
    patches = trans_ref.shape[1]
    high, low = split2(trans_ref[...])
    left_ref[:, 0:patches] = high.astype(BF16)
    left_ref[:, patches : 2 * patches] = high.astype(BF16)
    left_ref[:, 2 * patches : 3 * patches] = low.astype(BF16)
    light = force_ref[0:1, :]
    light = light / (light + 0.5)
    weights = [jnp.broadcast_to(weight_ref[t : t + 1, :], (patches, LANES)) for t in range(kinds)]
    half = 0.5 * light

    def one(k, above):
        mass = bio_ref[pl.ds(k, patches, stride=bins), :]
        leaf = mass * trait_ref[0, k]
        gain = trait_ref[1, k] * leaf * jnp.exp(-0.05 * above) * half
        grown = mass * (1.0 - 0.1 * trait_ref[2, k]) + gain
        high, low = split2(grown)
        high = high.astype(BF16)
        return jnp.concatenate([high, low.astype(BF16), high], axis=0), above + leaf

    def body(i, above):
        k = bins - 1 - 2 * i
        first, above = one(k, above)
        second, above = one(k - 1, above)
        right = jnp.concatenate([first, second], axis=1)
        moved = jnp.dot(left_ref[...], right, preferred_element_type=F32)
        for j in range(2):
            part = moved[:, j * LANES : (j + 1) * LANES]
            total = part[0:patches] * weights[0]
            for t in range(1, kinds):
                total = total + part[t * patches : (t + 1) * patches] * weights[t]
            out_ref[pl.ds(k - j, patches, stride=bins), :] = total
        return above

    lax.fori_loop(0, bins // 2, body, jnp.zeros((patches, LANES), F32), unroll=4)


def river_kernel(
    slots,
    here_ref,
    arrived_ref,
    target_ref,
    mate_ref,
    water_ref,
    rate_ref,
    out_ref,
    hill_out_ref,
    lo_ref,
    mask_ref,
    state_ref,
    speed_ref,
    value_ref,
    rows_left_ref,
    rows_lo_ref,
    hill_ref,
    hill_rate_ref,
    runoff_ref,
    sems,
):
    peers = arrived_ref.shape[0]
    chunks = state_ref.shape[1]
    spans = 2 * chunks
    window = state_ref.shape[0]
    base = here_ref[0]
    core = here_ref[1]
    other = 1 - core
    rows = target_ref.shape[0]

    def block_of(b):
        j = base + b
        return jnp.where(j >= peers, j - peers, j)

    square = (LANES, LANES)
    eye = jnp.where(row_iota(square) == lane_iota(square), 1.0, 0.0).astype(BF16)
    wide = (2 * LANES, 2 * LANES)
    ones = jnp.where(row_iota(wide) // LANES == lane_iota(wide) // LANES, 1.0, 0.0).astype(BF16)
    lane = lane_iota(square).astype(F32)

    def table(b, carry):
        j = block_of(b)
        target = arrived_ref[j, 0:chunks].astype(jnp.int32)
        span = target >> 7
        low = (target & 127).astype(F32)
        for h in range(0, chunks, 2):
            diagonal = jnp.concatenate(
                [
                    jnp.broadcast_to(low[h + i : h + i + 1, :], square).astype(BF16) * eye
                    for i in range(2)
                ],
                axis=1,
            )
            column = jnp.dot(diagonal, ones, preferred_element_type=F32)
            for i in range(2):
                at = slice((h + i) * LANES, (h + i + 1) * LANES)
                mask_ref[b, h + i] = jnp.where(
                    row_iota((spans, LANES)) == span[h + i : h + i + 1, :], 1.0, 0.0
                ).astype(BF16)
                lo_ref[b, at, :] = jnp.where(
                    column[:, i * LANES : (i + 1) * LANES] == lane, 1.0, 0.0
                ).astype(BF16)
        speed_ref[b] = arrived_ref[j, chunks:spans]
        return carry

    lax.fori_loop(0, window - 1, table, 0)

    arrived_rows_ref = arrived_ref.reshape(peers * arrived_ref.shape[1], LANES)
    fraction = 1.0 / NSUB
    half = 3 * chunks
    for which in range(2):
        if which == 0:
            target = target_ref[...]
        else:
            target = mate_ref[3 * chunks :, :].astype(jnp.int32)
        span = target >> 7
        low = target & 127
        values = [split2(from_peers(arrived_rows_ref, rows, slots, f, spans + which, arrived_ref.shape[1])) for f in range(3)]
        for a in range(rows):
            mask = row_iota((chunks, LANES)) == span[a : a + 1, :]
            for s in range(2):
                for f in range(3):
                    m = (s * 3 + f) * chunks
                    rows_left_ref[which, a, m : m + chunks, :] = jnp.where(
                        mask, values[f][s][a : a + 1, :], 0.0
                    ).astype(BF16)
            rows_lo_ref[which, a] = jnp.where(
                row_iota((LANES, LANES)) == low[a : a + 1, :], 1.0, 0.0
            ).astype(BF16)
        taken = nt_dot(
            jnp.concatenate([rows_left_ref[which, a] for a in range(rows)], axis=1),
            jnp.concatenate([rows_lo_ref[which, a] for a in range(rows)], axis=1),
        )
        for f in range(3):
            runoff_ref[which, f] = fraction * (
                taken[f * chunks : (f + 1) * chunks]
                + taken[half + f * chunks : half + (f + 1) * chunks]
            )

    state_ref[...] = jnp.zeros_like(state_ref)
    for q in range(2):
        hill_ref[q] = unrow(water_ref[q : q + 1, :], chunks)
        hill_rate_ref[q] = unrow(rate_ref[q : q + 1, :], chunks)
    own = jnp.where(core == 0, water_ref[2:3, :], water_ref[3:4, :])
    state_ref[core] = unrow(own, chunks)
    state_ref[other] = mate_ref[0:chunks, :]
    hill_ref[2] = mate_ref[chunks : 2 * chunks, :]
    hill_rate_ref[2] = mate_ref[2 * chunks : 3 * chunks, :]
    deep = [jnp.where(core == 0, runoff_ref[which, 2], 0.0) for which in range(2)]
    surface = [runoff_ref[0, 0], runoff_ref[0, 1], runoff_ref[1, core]]

    def block_flow(b):
        out = speed_ref[b] * state_ref[b]
        high, low = split2(out)
        value_ref[b, 0] = high
        value_ref[b, 1] = low
        pieces = []
        for h in range(chunks):
            mask = mask_ref[b, h]
            pieces.append(
                jnp.concatenate(
                    [
                        jnp.broadcast_to(value_ref[b, s, h : h + 1, :], (spans, LANES)).astype(BF16)
                        * mask
                        for s in range(2)
                    ],
                    axis=0,
                )
            )
        flow = jnp.dot(
            jnp.concatenate(pieces, axis=1), lo_ref[b], preferred_element_type=F32
        )
        return out, flow[0:spans] + flow[spans : 2 * spans]

    def advance(count):
        for b in reversed(range(count)):
            out, flow = block_flow(b)
            state_ref[b] = state_ref[b] - out + flow[0:chunks]
            state_ref[b + 1] += flow[chunks:spans]

    for phase in range(NSUB // PHASE):

        def step(t, carry):
            advance(phase * PHASE + PHASE + 1)
            gone = [hill_rate_ref[i] * hill_ref[i] for i in range(3)]
            for i in range(3):
                hill_ref[i] = hill_ref[i] - gone[i] + surface[i]
            state_ref[core] += jnp.where(core == 0, gone[0], gone[1]) + deep[0]
            state_ref[other] += gone[2] + deep[1]
            return carry

        lax.fori_loop(0, PHASE, step, 0)

    hill_out_ref[...] = hill_ref[0:2]

    def send(b):
        return pltpu.make_async_copy(state_ref.at[b], out_ref.at[block_of(b)], sems.at[b])

    for b in range(window):
        send(b).start()
    for b in range(window):
        send(b).wait()


def inundate_kernel(slots, window, here_ref, part_ref, capacity_ref, target_ref, hill_ref, state_ref, back_ref):
    peers = part_ref.shape[0]
    chunks = capacity_ref.shape[0]
    channel = [jnp.zeros(part_ref.shape[1:], F32)] * 2
    for b in range(0, window, 2):
        j = here_ref[0] - b
        j = jnp.where(j < 0, j + peers, j)
        for q in range(2):
            channel[q] = channel[q] + part_ref[j + q]
    for q in range(2):
        for h in range(chunks):
            at = slice(h * LANES, (h + 1) * LANES)
            state_ref[q : q + 1, at] = hill_ref[q, h : h + 1, :]
            state_ref[2 + q : 3 + q, at] = channel[q][h : h + 1, :]
    stored = channel[0] + channel[1]
    wet = stored / (stored + capacity_ref[...])
    target = by_peer(target_ref, peers, slots)
    span = target >> 7
    low = target & 127
    back = jnp.zeros((peers, LANES), F32)
    for h in range(chunks):
        taken = jnp.take_along_axis(
            jnp.broadcast_to(wet[h : h + 1, :], (peers, LANES)), low, axis=1, mode="promise_in_bounds"
        )
        back = jnp.where(span == h, taken, back)
    back_ref[...] = back


def survive_kernel(bins, slots, trait_ref, back_ref, share_ref, source_ref, moved_ref, out_ref, flooded_ref, alive_ref):
    @pl.when(pl.program_id(0) == 0)
    def _():
        rows = share_ref.shape[0]
        value = share_ref[...] * from_peers(back_ref, rows, slots)
        source = source_ref[...]
        total = jnp.zeros((LANES, LANES), F32)
        for a in range(rows):
            total = total + jnp.where(
                row_iota((LANES, LANES)) == source[a : a + 1, :], value[a : a + 1, :], 0.0
            )
        flooded = jnp.sum(total.T, axis=0, keepdims=True)
        flooded_ref[...] = flooded
        for k in range(bins):
            alive_ref[k : k + 1, :] = jnp.exp(-trait_ref[3, k] * flooded)

    alive = alive_ref[...]
    for p in range(moved_ref.shape[0] // bins):
        at = slice(p * bins, (p + 1) * bins)
        out_ref[at, :] = moved_ref[at, :] * alive


def shards(
    axes,
    biomass,
    patch_area,
    cohort_traits,
    cell_forcing,
    disturb_weight,
    transitions,
    land_source,
    pair_share,
    river_target,
    downstream_step,
    river_water,
    river_rates,
    capacity,
):
    patches, bins, lands = biomass.shape
    rivers = river_water.shape[1]
    peers = math.prod(lax.axis_size(a) for a in axes)
    slots = land_source.shape[0] // peers
    rows = land_source.shape[0] // LANES
    chunks = rivers // LANES
    kinds = transitions.shape[0]
    window = NSUB + 2
    place = lax.axis_index(axes).astype(jnp.int32)
    here = jnp.stack([place - place % 2, place % 2])

    bio = biomass.reshape(patches * bins, lands)
    source = land_source.reshape(rows, LANES)
    share = pair_share.reshape(rows, LANES)
    target = river_target.reshape(rows, LANES)
    step = downstream_step.reshape(chunks, LANES)

    tile = 16
    whole = lambda *shape: pl.BlockSpec(shape, lambda i: (0,) * len(shape))
    message, mate = pl.pallas_call(
        functools.partial(rain_kernel, bins, slots),
        grid=(patches // tile,),
        out_shape=(
            jax.ShapeDtypeStruct((peers, 2 * chunks + 8, LANES), F32),
            jax.ShapeDtypeStruct((3 * chunks + rows, LANES), F32),
        ),
        in_specs=[
            SMEM,
            SMEM,
            pl.BlockSpec((tile * bins, LANES), lambda i: (i, 0)),
            pl.BlockSpec((tile, LANES), lambda i: (i, 0)),
            whole(5, LANES),
            whole(rows, LANES),
            whole(rows, LANES),
            whole(chunks, LANES),
            whole(rows, LANES),
            whole(4, rivers),
            whole(4, rivers),
        ],
        out_specs=(ANY, whole(3 * chunks + rows, LANES)),
        scratch_shapes=[
            pltpu.VMEM((1, LANES), F32),
            pltpu.VMEM((2, 2 * chunks, LANES), F32),
            pltpu.VMEM((peers * 8, LANES), F32),
            pltpu.SemaphoreType.DMA((peers,)),
            pltpu.SemaphoreType.DMA(()),
        ],
        name="rain",
    )(
        here[1:2],
        cohort_traits,
        bio,
        patch_area,
        cell_forcing,
        source,
        share,
        step,
        target,
        river_water,
        river_rates,
    )
    arrived = lax.all_to_all(message, axes, split_axis=0, concat_axis=0, tiled=True)
    mate = lax.ppermute(mate, axes, [(i, i + 1 - 2 * (i % 2)) for i in range(peers)])

    moved = pl.pallas_call(
        functools.partial(transit_kernel, kinds, bins),
        out_shape=jax.ShapeDtypeStruct((patches * bins, LANES), F32),
        in_specs=[SMEM, VMEM, VMEM, VMEM, VMEM],
        out_specs=VMEM,
        scratch_shapes=[pltpu.VMEM((kinds * patches, 3 * patches), BF16)],
        name="transit",
    )(cohort_traits, transitions.reshape(kinds * patches, patches), bio, cell_forcing, disturb_weight)

    spans = 2 * chunks
    parts, hill = pl.pallas_call(
        functools.partial(river_kernel, slots),
        out_shape=(
            jax.ShapeDtypeStruct((peers, chunks, LANES), F32),
            jax.ShapeDtypeStruct((2, chunks, LANES), F32),
        ),
        in_specs=[SMEM] + [VMEM] * 5,
        out_specs=(ANY, VMEM),
        scratch_shapes=[
            pltpu.VMEM((window - 1, rivers, LANES), BF16),
            pltpu.VMEM((window - 1, chunks, spans, LANES), BF16),
            pltpu.VMEM((window, chunks, LANES), F32),
            pltpu.VMEM((window - 1, chunks, LANES), F32),
            pltpu.VMEM((window - 1, 2, chunks, LANES), F32),
            pltpu.VMEM((2, rows, 6 * chunks, LANES), BF16),
            pltpu.VMEM((2, rows, LANES, LANES), BF16),
            pltpu.VMEM((3, chunks, LANES), F32),
            pltpu.VMEM((3, chunks, LANES), F32),
            pltpu.VMEM((2, 3, chunks, LANES), F32),
            pltpu.SemaphoreType.DMA((window,)),
        ],
        name="river",
    )(here, arrived, target, mate, river_water, river_rates)
    parts = lax.all_to_all(parts, axes, split_axis=0, concat_axis=0, tiled=True)

    river_state, back = pl.pallas_call(
        functools.partial(inundate_kernel, slots, window),
        out_shape=(
            jax.ShapeDtypeStruct((4, rivers), F32),
            jax.ShapeDtypeStruct((peers, LANES), F32),
        ),
        in_specs=[SMEM] + [VMEM] * 4,
        out_specs=(VMEM, VMEM),
        name="inundate",
    )(here, parts, capacity.reshape(chunks, LANES), target, hill)
    back = lax.all_to_all(back, axes, split_axis=0, concat_axis=0, tiled=True)

    tile = 12
    new_biomass, flooded = pl.pallas_call(
        functools.partial(survive_kernel, bins, slots),
        grid=(patches // tile,),
        out_shape=(
            jax.ShapeDtypeStruct((patches * bins, LANES), F32),
            jax.ShapeDtypeStruct((1, LANES), F32),
        ),
        in_specs=[
            SMEM,
            pl.BlockSpec((peers, LANES), lambda i: (0, 0)),
            pl.BlockSpec((rows, LANES), lambda i: (0, 0)),
            pl.BlockSpec((rows, LANES), lambda i: (0, 0)),
            pl.BlockSpec((tile * bins, LANES), lambda i: (i, 0)),
        ],
        out_specs=(
            pl.BlockSpec((tile * bins, LANES), lambda i: (i, 0)),
            pl.BlockSpec((1, LANES), lambda i: (0, 0)),
        ),
        scratch_shapes=[pltpu.VMEM((bins, LANES), F32)],
        name="survive",
    )(cohort_traits, back, share, source, moved)
    return (new_biomass.reshape(patches, bins, lands), flooded.reshape(lands), river_state)


def solution(mesh):
    axes = tuple(mesh.axis_names)
    split = P(axes)
    split1 = P(None, axes)

    def body(*args):
        return shards(axes, *args)

    return jax.shard_map(
        body,
        mesh=mesh,
        in_specs=(
            P(None, None, axes),
            split1,
            P(),
            split1,
            split1,
            P(),
            split,
            split,
            split,
            split,
            split1,
            split1,
            split,
        ),
        out_specs=(P(None, None, axes), split, split1),
        check_vma=False,
    )
```

time: 106 us -> 81 us (0.76)
  waiting for transfers between devices: 27.1 us -> 18.1 us
  Pallas kernels: 44.5 us -> 35.9 us
  blocking collectives: 19.5 us -> 13.3 us
  starting transfers between devices: 12.5 us -> 10.4 us
    all_to_all x1 -> x0, waiting for transfers between devices: 21.8 us -> none  [shards(): lax.all_to_all(statics, axes, split_axis=0, concat_axis=0, tiled=True)]
    all_to_all x1, waiting for transfers between devices: 5.25 us -> 17.6 us  [shards(): lax.all_to_all(message, axes, split_axis=0, concat_axis=0, tiled=True)]
    pallas_call x1, Pallas kernels: 26 us -> 18.3 us  [shards(): pl.pallas_call(functools.partial(river_kernel, slots), out_shape=(jax.Sha...]
    all_to_all x1, blocking collectives: 19.5 us -> 13.3 us  [shards(): parts = lax.all_to_all(parts, axes, split_axis=0, concat_axis=0, tiled=True)]
    all_to_all x1 -> x0, starting transfers between devices: 2.63 us -> none  [shards(): lax.all_to_all(statics, axes, split_axis=0, concat_axis=0, tiled=True)]
    pallas_call x1 -> x0, Pallas kernels: 1.85 us -> none  [shards(): pl.pallas_call(statics_kernel, out_shape=jax.ShapeDtypeStruct((peers, 3,...]
  transfers between devices with their start and end apart: 3 -> 3, of which waited for: 2 -> 2; matrix products, arithmetic and copies ran while one was open for 0% -> 1% of each run, Pallas kernels for 9% -> 9%
where the time goes in v2:
time: 81 us; the launch traced here: 80.5 us
  Pallas kernels  35.9 us (44%)
  waiting for transfers between devices  18.1 us (22%)
  blocking collectives  13.3 us (16%)
  starting transfers between devices  10.4 us (13%)
  local copies, waits for them, and re-layouts  1.44 us (2%)
    pallas_call x1, Pallas kernels, shards(): pl.pallas_call(functools.partial(river_kernel, slots), out_shape=(jax.Sha...  18.3 us
    all_to_all x1, waiting for transfers between devices, shards(): lax.all_to_all(message, axes, split_axis=0, concat_axis=0, tiled=True)  17.6 us
    all_to_all x1, blocking collectives, shards(): parts = lax.all_to_all(parts, axes, split_axis=0, concat_axis=0, tiled=True)  13.3 us
    all_to_all x1, starting transfers between devices, shards(): lax.all_to_all(message, axes, split_axis=0, concat_axis=0, tiled=True)  7.33 us
    pallas_call x1, Pallas kernels, shards(): pl.pallas_call(functools.partial(transit_kernel, kinds, bins), out_shape=...  7.28 us
    pallas_call x1, Pallas kernels, shards(): pl.pallas_call(functools.partial(rain_kernel, bins, slots), grid=(patches...  4.71 us
    pallas_call x1, Pallas kernels, shards(): pl.pallas_call(functools.partial(survive_kernel, bins, slots), grid=(patc...  3.77 us
    all_to_all x1, starting transfers between devices, shards(): back = lax.all_to_all(back, axes, split_axis=0, concat_axis=0, tiled=True)  2.78 us
  transfers between devices with their start and end apart: 3, of which 2 were waited for; matrix products, arithmetic and copies ran while one was open for 1% of the time, Pallas kernels for 9%

profile of v2, /device:TPU:0, one launch (start us, length us, event | category | flops | bytes accessed | tf_op | source)
XLA Modules:
  0.0 80.5 jit_solution(8613013248027217318)
XLA Ops:
  0.6 4.7 %rain.1 = (f32[32,40,128]{2,1,0:T(8,128)}, f32[56,128]{1,0:T(8,128)}) custom-call(s32[1]{0:T(128)} %bitcast.1.core_ref, f32[4,64]{1,0:T(4,128)} %trait_ref.5, f32[3072,128]{1,0:T(8,128)} %bitcast.15, f32[48,128]{1,0:T(8,128)} %area_ref.1, f32[5,128]{1,0:T(8,128)} %force_ref.3, s32[8,128]{1,0:T(8,128)} %bitcast.22, f32[8,128]{1,0:T(8,128)} %bitcast.24, ...), custom_call_target="tpu_custom_call" | custom-call | tf_op jit(solution)/shard_map/rain/pallas_call | solution.py:453
  5.4 7.3 %all-to-all-start = ((f32[32,40,128]{2,1,0:T(8,128)}), f32[32,40,128]{2,1,0:T(8,128)S(1)}, u32[]{:S(2)}, u32[]{:S(2)}) async-start(f32[32,40,128]{2,1,0:T(8,128)} %get-tuple-element.11), calls=%async_computation | async-start | bytes 1310720 | tf_op jit(solution)/shard_map/all_to_all | solution.py:495
  12.7 0.3 collective-permute-start
  13.0 0.6 pad_add_fusion.here_ref
  13.6 0.6 collective-permute-done.mate_ref
  14.2 0.0 copy-start.2
  14.2 17.6 %all-to-all-done.arrived_ref = f32[32,40,128]{2,1,0:T(8,128)S(1)} async-done(((f32[32,40,128]{2,1,0:T(8,128)}), f32[32,40,128]{2,1,0:T(8,128)S(1)}, u32[]{:S(2)}, u32[]{:S(2)}) %all-to-all-start) | async-done | bytes 655392 | tf_op jit(solution)/shard_map/all_to_all | solution.py:495
  31.7 0.0 copy-done.2
  31.7 0.0 copy-start
  31.8 0.8 %copy-done = f32[32,40,128]{2,1,0:T(8,128)} copy-done((f32[32,40,128]{2,1,0:T(8,128)}, f32[32,40,128]{2,1,0:T(8,128)S(1)}, u32[]{:S(2)}) %copy-start) | copy-done | bytes 655384
  32.6 18.3 %river.1 = (f32[32,16,128]{2,1,0:T(8,128)}, f32[2,16,128]{2,1,0:T(8,128)}) custom-call(s32[2]{0:T(128)} %pad_add_fusion.here_ref, f32[32,40,128]{2,1,0:T(8,128)} %copy-done, s32[8,128]{1,0:T(8,128)} %bitcast.20, f32[56,128]{1,0:T(8,128)} %copy-done.2, f32[4,2048]{1,0:T(4,128)} %water_ref.3, f32[4,2048]{1,0:T(4,128)} %rate_ref.3), custom_call_target="tpu_custom_call" | custom-call | tf_op jit(solution)/shard_map/river/pallas_call | solution.py:508
  50.9 13.3 %all_to_all.21.part_ref = f32[32,16,128]{2,1,0:T(8,128)} all-to-all(f32[32,16,128]{2,1,0:T(8,128)} %get-tuple-element.13), channel_id=1, replica_groups=mesh['comp'=4,'cell'=8] {'comp','cell'}, dimensions={0} | all-to-all | bytes 524288 | tf_op jit(solution)/shard_map/all_to_all | solution.py:531
  64.2 1.9 %inundate.1 = (f32[4,2048]{1,0:T(4,128)}, f32[32,128]{1,0:T(8,128)}) custom-call(s32[2]{0:T(128)} %pad_add_fusion.here_ref, f32[32,16,128]{2,1,0:T(8,128)} %all_to_all.21.part_ref, f32[16,128]{1,0:T(8,128)} %bitcast.28, s32[8,128]{1,0:T(8,128)} %bitcast.21, f32[2,16,128]{2,1,0:T(8,128)} %get-tuple-element.14.hill_ref), custom_call_target="tpu_custom_call" | custom-call | tf_op jit(solution)/shard_map/inundate/pallas_call | solution.py:533
  66.1 2.8 %all-to-all-start.2 = ((f32[32,1,128]{2,1,0:T(1,128)}), f32[32,1,128]{2,1,0:T(1,128)S(1)}, u32[]{:S(2)}, u32[]{:S(2)}) async-start(f32[32,1,128]{2,1,0:T(1,128)} %bitcast.26), calls=%async_computation.2 | async-start | bytes 32768 | tf_op jit(solution)/shard_map/all_to_all | solution.py:543
  68.9 7.3 %transit.1.moved_ref = f32[3072,128]{1,0:T(8,128)} custom-call(f32[4,64]{1,0:T(4,128)} %trait_ref.5, f32[192,48]{1,0:T(8,128)} %bitcast.17, f32[3072,128]{1,0:T(8,128)} %bitcast.16, f32[5,128]{1,0:T(8,128)} %force_ref.3, f32[4,128]{1,0:T(4,128)} %weight_ref.1), custom_call_target="tpu_custom_call" | custom-call | tf_op jit(solution)/shard_map/transit/pallas_call | solution.py:498
  76.1 0.0 all-to-all-done.2
  76.1 0.0 copy-start.1
  76.1 0.6 copy-done.1
  76.7 3.8 %survive.1 = (f32[3072,128]{1,0:T(8,128)}, f32[1,128]{1,0:T(1,128)}) custom-call(f32[4,64]{1,0:T(4,128)} %trait_ref.5, f32[32,128]{1,0:T(8,128)} %bitcast.18, f32[8,128]{1,0:T(8,128)} %bitcast.25, s32[8,128]{1,0:T(8,128)} %bitcast.23, f32[3072,128]{1,0:T(8,128)} %transit.1.moved_ref), custom_call_target="tpu_custom_call" | custom-call | tf_op jit(solution)/shard_map/survive/pallas_call | solution.py:546
Async XLA Ops:
  5.4 26.4 %all-to-all-start = ((f32[32,40,128]{2,1,0:T(8,128)}), f32[32,40,128]{2,1,0:T(8,128)S(1)}, u32[]{:S(2)}, u32[]{:S(2)}) async-start(f32[32,40,128]{2,1,0:T(8,128)} %get-tuple-element.11), calls=%async_computation | async-start | bytes 1310720 | tf_op jit(solution)/shard_map/all_to_all | solution.py:495
  12.7 1.5 %collective-permute-start = (f32[56,128]{1,0:T(8,128)}, f32[56,128]{1,0:T(8,128)S(1)}, u32[]{:S(2)}, u32[]{:S(2)}) collective-permute-start(f32[56,128]{1,0:T(8,128)} %get-tuple-element.12), channel_id=1, source_target_pairs={{0,1},{1,0},{2,3},{3,2},{4,5},{5,4},{6,7},{7,6},{8,9},{9,8},{10,11... | collective-permute-start | bytes 86024 | tf_op jit(solution)/shard_map/ppermute | solution.py:496
  14.2 17.6 %copy-start.2 = (f32[56,128]{1,0:T(8,128)}, f32[56,128]{1,0:T(8,128)S(1)}, u32[]{:S(2)}) copy-start(f32[56,128]{1,0:T(8,128)S(1)} %collective-permute-done.mate_ref) | copy-start | bytes 86020
  31.7 0.8 %copy-start = (f32[32,40,128]{2,1,0:T(8,128)}, f32[32,40,128]{2,1,0:T(8,128)S(1)}, u32[]{:S(2)}) copy-start(f32[32,40,128]{2,1,0:T(8,128)S(1)} %all-to-all-done.arrived_ref) | copy-start | bytes 1966084
  66.1 10.1 %all-to-all-start.2 = ((f32[32,1,128]{2,1,0:T(1,128)}), f32[32,1,128]{2,1,0:T(1,128)S(1)}, u32[]{:S(2)}, u32[]{:S(2)}) async-start(f32[32,1,128]{2,1,0:T(1,128)} %bitcast.26), calls=%async_computation.2 | async-start | bytes 32768 | tf_op jit(solution)/shard_map/all_to_all | solution.py:543
  76.1 0.6 copy-start.1

commit v3 on v2

--- a/solution.py
+++ b/solution.py
@@ -37,10 +37,9 @@
     return high, x - high
 
 
-def by_peer(ref, peers, slots):
-    rows = ref.shape[0]
+def by_peer(value, peers, slots):
+    rows = value.shape[0]
     per = peers // rows
-    value = ref[...]
     spread = jnp.concatenate(
         [jnp.broadcast_to(value[a : a + 1, :], (per, LANES)) for a in range(rows)], axis=0
     )
@@ -61,6 +60,26 @@
             if shift:
                 part = pltpu.roll(part, shift, 1)
         out = jnp.where(section == b, part, out)
+    return out
+
+
+def all_sections(value, slots):
+    shift = slots
+    while shift < LANES:
+        value = value + pltpu.roll(value, shift, 1)
+        shift *= 2
+    return value
+
+
+def look_up(table, index):
+    span = index >> 7
+    low = index & 127
+    out = jnp.zeros(index.shape, F32)
+    for h in range(table.shape[0]):
+        taken = jnp.take_along_axis(
+            jnp.broadcast_to(table[h : h + 1, :], index.shape), low, axis=1, mode="promise_in_bounds"
+        )
+        out = jnp.where(span == h, taken, out)
     return out
 
 
@@ -82,25 +101,19 @@
     target_ref,
     water_ref,
     rate_ref,
+    capacity_ref,
     out_ref,
     mate_ref,
     total_ref,
-    static_ref,
-    rows_ref,
-    sems,
-    rows_sem,
 ):
     step = pl.program_id(0)
     patches = area_ref.shape[0]
-    peers = out_ref.shape[0]
     chunks = step_ref.shape[0]
+    rows = target_ref.shape[0]
+    size = 2 * chunks + rows + 2
+    peers = out_ref.shape[0] // size
     light = force_ref[0:1, :]
     light = light / (light + 0.5)
-
-    def spread(j):
-        return pltpu.make_async_copy(
-            static_ref.at[j % 2], out_ref.at[j, pl.ds(0, 2 * chunks)], sems.at[j]
-        )
 
     @pl.when(step == 0)
     def _():
@@ -109,16 +122,18 @@
         moves = step_ref[...]
         cell = row_iota(shape) * LANES + lane_iota(shape)
         target = jnp.where(moves > 0, cell + moves, -1).astype(F32)
-        for q in range(2):
-            static_ref[q, 0:chunks, :] = target
-            static_ref[q, chunks : 2 * chunks, :] = unrow(rate_ref[2 + q : 3 + q, :], chunks)
+        rates = [unrow(rate_ref[2 + q : 3 + q, :], chunks) for q in range(2)]
+        land = target_ref[...].astype(F32)
         for j in range(peers):
-            spread(j).start()
+            at = size * j
+            out_ref[at : at + chunks, :] = target
+            out_ref[at + chunks : at + 2 * chunks, :] = rates[j % 2]
+            out_ref[at + 2 * chunks : at + 2 * chunks + rows, :] = land
         first = core_ref[0] == 0
         for i, (ref, at) in enumerate(((water_ref, 2), (water_ref, 0), (rate_ref, 0))):
             other = jnp.where(first, ref[at + 1 : at + 2, :], ref[at : at + 1, :])
             mate_ref[i * chunks : (i + 1) * chunks, :] = unrow(other, chunks)
-        mate_ref[3 * chunks :, :] = target_ref[...].astype(F32)
+        mate_ref[3 * chunks :, :] = land
 
     above = jnp.zeros((patches, LANES), F32)
     total = jnp.zeros((patches, LANES), F32)
@@ -138,8 +153,8 @@
             wet * frozen,
             force_ref[3:4, :] * jnp.exp(-0.5 * (0.5 * total_ref[...])),
         ]
-        source = by_peer(source_ref, peers, slots)
-        share = by_peer(share_ref, peers, slots)
+        source = by_peer(source_ref[...], peers, slots)
+        share = by_peer(share_ref[...], peers, slots)
         safe = jnp.maximum(source, 0)
         section = lane_iota(shape) // slots
         value = jnp.zeros(shape, F32)
@@ -152,15 +167,9 @@
         mate = jnp.where(
             row_iota(shape) % 2 == 0, pltpu.roll(own, peers - 1, 0), pltpu.roll(own, 1, 0)
         )
-        rows_ref[pl.ds(0, peers, stride=8), :] = own
-        rows_ref[pl.ds(1, peers, stride=8), :] = mate
-        copy = pltpu.make_async_copy(
-            rows_ref.reshape(peers, 8, LANES), out_ref.at[:, pl.ds(2 * chunks, 8)], rows_sem
-        )
-        copy.start()
-        for j in range(peers):
-            spread(j).wait()
-        copy.wait()
+        room = by_peer(look_up(capacity_ref[...], target_ref[...]), peers, slots)
+        out_ref[pl.ds(size - 2, peers, stride=size), :] = jnp.where(section == 3, room, own)
+        out_ref[pl.ds(size - 1, peers, stride=size), :] = mate
 
 
 def transit_kernel(kinds, bins, trait_ref, trans_ref, bio_ref, force_ref, weight_ref, out_ref, left_ref):
@@ -210,6 +219,7 @@
     rate_ref,
     out_ref,
     hill_out_ref,
+    room_ref,
     lo_ref,
     mask_ref,
     state_ref,
@@ -220,16 +230,16 @@
     hill_ref,
     hill_rate_ref,
     runoff_ref,
-    sems,
 ):
-    peers = arrived_ref.shape[0]
     chunks = state_ref.shape[1]
+    rows = target_ref.shape[0]
+    size = 2 * chunks + rows + 2
+    peers = arrived_ref.shape[0] // size
     spans = 2 * chunks
     window = state_ref.shape[0]
     base = here_ref[0]
     core = here_ref[1]
     other = 1 - core
-    rows = target_ref.shape[0]
 
     def block_of(b):
         j = base + b
@@ -243,7 +253,7 @@
 
     def table(b, carry):
         j = block_of(b)
-        target = arrived_ref[j, 0:chunks].astype(jnp.int32)
+        target = arrived_ref[pl.ds(j * size, chunks), :].astype(jnp.int32)
         span = target >> 7
         low = (target & 127).astype(F32)
         for h in range(0, chunks, 2):
@@ -263,12 +273,11 @@
                 lo_ref[b, at, :] = jnp.where(
                     column[:, i * LANES : (i + 1) * LANES] == lane, 1.0, 0.0
                 ).astype(BF16)
-        speed_ref[b] = arrived_ref[j, chunks:spans]
+        speed_ref[b] = arrived_ref[pl.ds(j * size + chunks, chunks), :]
         return carry
 
     lax.fori_loop(0, window - 1, table, 0)
 
-    arrived_rows_ref = arrived_ref.reshape(peers * arrived_ref.shape[1], LANES)
     fraction = 1.0 / NSUB
     half = 3 * chunks
     for which in range(2):
@@ -278,7 +287,7 @@
             target = mate_ref[3 * chunks :, :].astype(jnp.int32)
         span = target >> 7
         low = target & 127
-        values = [split2(from_peers(arrived_rows_ref, rows, slots, f, spans + which, arrived_ref.shape[1])) for f in range(3)]
+        values = [split2(from_peers(arrived_ref, rows, slots, f, size - 2 + which, size)) for f in range(3)]
         for a in range(rows):
             mask = row_iota((chunks, LANES)) == span[a : a + 1, :]
             for s in range(2):
@@ -356,48 +365,79 @@
 
     hill_out_ref[...] = hill_ref[0:2]
 
-    def send(b):
-        return pltpu.make_async_copy(state_ref.at[b], out_ref.at[block_of(b)], sems.at[b])
-
+    shape = (peers, LANES)
+    section = lane_iota(shape) // slots
+    room = arrived_ref[pl.ds(size - 2, peers, stride=size), :]
+    room_ref[...] = all_sections(jnp.where(section == 3, room, 0.0), slots)
+
+    extra = -(-window * slots // LANES)
+    out_size = chunks + extra
+    reached = [jnp.zeros(shape, F32) for _ in range(extra)]
     for b in range(window):
-        send(b).start()
-    for b in range(window):
-        send(b).wait()
-
-
-def inundate_kernel(slots, window, here_ref, part_ref, capacity_ref, target_ref, hill_ref, state_ref, back_ref):
-    peers = part_ref.shape[0]
-    chunks = capacity_ref.shape[0]
-    channel = [jnp.zeros(part_ref.shape[1:], F32)] * 2
-    for b in range(0, window, 2):
-        j = here_ref[0] - b
-        j = jnp.where(j < 0, j + peers, j)
-        for q in range(2):
-            channel[q] = channel[q] + part_ref[j + q]
-    for q in range(2):
-        for h in range(chunks):
-            at = slice(h * LANES, (h + 1) * LANES)
-            state_ref[q : q + 1, at] = hill_ref[q, h : h + 1, :]
-            state_ref[2 + q : 3 + q, at] = channel[q][h : h + 1, :]
-    stored = channel[0] + channel[1]
-    wet = stored / (stored + capacity_ref[...])
-    target = by_peer(target_ref, peers, slots)
-    span = target >> 7
-    low = target & 127
-    back = jnp.zeros((peers, LANES), F32)
-    for h in range(chunks):
-        taken = jnp.take_along_axis(
-            jnp.broadcast_to(wet[h : h + 1, :], (peers, LANES)), low, axis=1, mode="promise_in_bounds"
-        )
-        back = jnp.where(span == h, taken, back)
-    back_ref[...] = back
-
-
-def survive_kernel(bins, slots, trait_ref, back_ref, share_ref, source_ref, moved_ref, out_ref, flooded_ref, alive_ref):
+        j = block_of(b)
+        out_ref[pl.ds(j * out_size, chunks), :] = state_ref[b]
+        index = arrived_ref[pl.ds(j * size + spans, rows), :].astype(jnp.int32)
+        value = by_peer(look_up(state_ref[b], index), peers, slots)
+        e, at = divmod(b * slots, LANES)
+        reached[e] = jnp.where(section == at // slots, value, reached[e])
+    for e in range(extra):
+        out_ref[pl.ds(chunks + e, peers, stride=out_size), :] = reached[e]
+
+
+def survive_kernel(
+    bins,
+    slots,
+    window,
+    here_ref,
+    trait_ref,
+    part_ref,
+    hill_ref,
+    room_ref,
+    share_ref,
+    source_ref,
+    moved_ref,
+    out_ref,
+    flooded_ref,
+    state_ref,
+    alive_ref,
+    wet_ref,
+):
+    peers = room_ref.shape[0]
+    chunks = hill_ref.shape[1]
+    size = part_ref.shape[0] // peers
+
     @pl.when(pl.program_id(0) == 0)
     def _():
+        channel = [jnp.zeros((chunks, LANES), F32)] * 2
+        for b in range(0, window, 2):
+            j = here_ref[0] - b
+            j = jnp.where(j < 0, j + peers, j)
+            for q in range(2):
+                channel[q] = channel[q] + part_ref[pl.ds((j + q) * size, chunks), :]
+        for q in range(2):
+            for h in range(chunks):
+                at = slice(h * LANES, (h + 1) * LANES)
+                state_ref[q : q + 1, at] = hill_ref[q, h : h + 1, :]
+                state_ref[2 + q : 3 + q, at] = channel[q][h : h + 1, :]
+
+        shape = (peers, LANES)
+        section = lane_iota(shape) // slots
+        even = row_iota(shape) % 2 == 0
+        stored = jnp.zeros(shape, F32)
+        for e in range(size - chunks):
+            part = part_ref[pl.ds(chunks + e, peers, stride=size), :]
+            part = part + jnp.where(even, pltpu.roll(part, peers - 1, 0), pltpu.roll(part, 1, 0))
+            for b in range(window):
+                if b * slots // LANES != e:
+                    continue
+                moved = pltpu.roll(part, b, 0) if b else part
+                mine = (section == b * slots % LANES // slots) & (even == (b % 2 == 0))
+                stored = stored + jnp.where(mine, moved, 0.0)
+        stored = all_sections(stored, slots)
+        wet_ref[...] = stored / (stored + room_ref[...])
+
         rows = share_ref.shape[0]
-        value = share_ref[...] * from_peers(back_ref, rows, slots)
+        value = share_ref[...] * from_peers(wet_ref, rows, slots)
         source = source_ref[...]
         total = jnp.zeros((LANES, LANES), F32)
         for a in range(rows):
@@ -448,13 +488,20 @@
     target = river_target.reshape(rows, LANES)
     step = downstream_step.reshape(chunks, LANES)
 
+    def exchange(message, size):
+        inner = math.gcd(size, 8)
+        message = message.reshape(peers, size // inner, inner, LANES)
+        arrived = lax.all_to_all(message, axes, split_axis=0, concat_axis=0, tiled=True)
+        return arrived.reshape(peers * size, LANES)
+
+    size = 2 * chunks + rows + 2
     tile = 16
     whole = lambda *shape: pl.BlockSpec(shape, lambda i: (0,) * len(shape))
     message, mate = pl.pallas_call(
         functools.partial(rain_kernel, bins, slots),
         grid=(patches // tile,),
         out_shape=(
-            jax.ShapeDtypeStruct((peers, 2 * chunks + 8, LANES), F32),
+            jax.ShapeDtypeStruct((peers * size, LANES), F32),
             jax.ShapeDtypeStruct((3 * chunks + rows, LANES), F32),
         ),
         in_specs=[
@@ -469,15 +516,10 @@
             whole(rows, LANES),
             whole(4, rivers),
             whole(4, rivers),
+            whole(chunks, LANES),
         ],
-        out_specs=(ANY, whole(3 * chunks + rows, LANES)),
-        scratch_shapes=[
-            pltpu.VMEM((1, LANES), F32),
-            pltpu.VMEM((2, 2 * chunks, LANES), F32),
-            pltpu.VMEM((peers * 8, LANES), F32),
-            pltpu.SemaphoreType.DMA((peers,)),
-            pltpu.SemaphoreType.DMA(()),
-        ],
+        out_specs=(whole(peers * size, LANES), whole(3 * chunks + rows, LANES)),
+        scratch_shapes=[pltpu.VMEM((1, LANES), F32)],
         name="rain",
     )(
         here[1:2],
@@ -491,8 +533,9 @@
         target,
         river_water,
         river_rates,
+        capacity.reshape(chunks, LANES),
     )
-    arrived = lax.all_to_all(message, axes, split_axis=0, concat_axis=0, tiled=True)
+    arrived = exchange(message, size)
     mate = lax.ppermute(mate, axes, [(i, i + 1 - 2 * (i % 2)) for i in range(peers)])
 
     moved = pl.pallas_call(
@@ -505,14 +548,16 @@
     )(cohort_traits, transitions.reshape(kinds * patches, patches), bio, cell_forcing, disturb_weight)
 
     spans = 2 * chunks
-    parts, hill = pl.pallas_call(
+    out_size = chunks - (-window * slots // LANES)
+    parts, hill, room = pl.pallas_call(
         functools.partial(river_kernel, slots),
         out_shape=(
-            jax.ShapeDtypeStruct((peers, chunks, LANES), F32),
+            jax.ShapeDtypeStruct((peers * out_size, LANES), F32),
             jax.ShapeDtypeStruct((2, chunks, LANES), F32),
+            jax.ShapeDtypeStruct((peers, LANES), F32),
         ),
         in_specs=[SMEM] + [VMEM] * 5,
-        out_specs=(ANY, VMEM),
+        out_specs=(VMEM, VMEM, VMEM),
         scratch_shapes=[
             pltpu.VMEM((window - 1, rivers, LANES), BF16),
             pltpu.VMEM((window - 1, chunks, spans, LANES), BF16),
@@ -524,46 +569,38 @@
             pltpu.VMEM((3, chunks, LANES), F32),
             pltpu.VMEM((3, chunks, LANES), F32),
             pltpu.VMEM((2, 3, chunks, LANES), F32),
-            pltpu.SemaphoreType.DMA((window,)),
         ],
         name="river",
     )(here, arrived, target, mate, river_water, river_rates)
-    parts = lax.all_to_all(parts, axes, split_axis=0, concat_axis=0, tiled=True)
-
-    river_state, back = pl.pallas_call(
-        functools.partial(inundate_kernel, slots, window),
-        out_shape=(
-            jax.ShapeDtypeStruct((4, rivers), F32),
-            jax.ShapeDtypeStruct((peers, LANES), F32),
-        ),
-        in_specs=[SMEM] + [VMEM] * 4,
-        out_specs=(VMEM, VMEM),
-        name="inundate",
-    )(here, parts, capacity.reshape(chunks, LANES), target, hill)
-    back = lax.all_to_all(back, axes, split_axis=0, concat_axis=0, tiled=True)
+    parts = exchange(parts, out_size)
 
     tile = 12
-    new_biomass, flooded = pl.pallas_call(
-        functools.partial(survive_kernel, bins, slots),
+    new_biomass, flooded, river_state = pl.pallas_call(
+        functools.partial(survive_kernel, bins, slots, window),
         grid=(patches // tile,),
         out_shape=(
             jax.ShapeDtypeStruct((patches * bins, LANES), F32),
             jax.ShapeDtypeStruct((1, LANES), F32),
+            jax.ShapeDtypeStruct((4, rivers), F32),
         ),
         in_specs=[
             SMEM,
-            pl.BlockSpec((peers, LANES), lambda i: (0, 0)),
-            pl.BlockSpec((rows, LANES), lambda i: (0, 0)),
-            pl.BlockSpec((rows, LANES), lambda i: (0, 0)),
+            SMEM,
+            whole(peers * out_size, LANES),
+            whole(2, chunks, LANES),
+            whole(peers, LANES),
+            whole(rows, LANES),
+            whole(rows, LANES),
             pl.BlockSpec((tile * bins, LANES), lambda i: (i, 0)),
         ],
         out_specs=(
             pl.BlockSpec((tile * bins, LANES), lambda i: (i, 0)),
-            pl.BlockSpec((1, LANES), lambda i: (0, 0)),
+            whole(1, LANES),
+            whole(4, rivers),
         ),
-        scratch_shapes=[pltpu.VMEM((bins, LANES), F32)],
+        scratch_shapes=[pltpu.VMEM((bins, LANES), F32), pltpu.VMEM((peers, LANES), F32)],
         name="survive",
-    )(cohort_traits, back, share, source, moved)
+    )(here, cohort_traits, parts, hill, room, share, source, moved)
     return (new_biomass.reshape(patches, bins, lands), flooded.reshape(lands), river_state)
 
 

time: 81 us -> 71.4 us (0.88)
  blocking collectives: 13.3 us -> 0 us
  waiting for transfers between devices: 18.1 us -> 23.6 us
  Pallas kernels: 35.9 us -> 34.3 us
    all_to_all x1 -> x0, blocking collectives: 13.3 us -> none  [shards(): parts = lax.all_to_all(parts, axes, split_axis=0, concat_axis=0, tiled=True)]
    all_to_all x2, waiting for transfers between devices: 17.6 us -> 23 us  [exchange(): lax.all_to_all(message, axes, split_axis=0, concat_axis=0, tiled=True)]
    pallas_call x2 -> x1, Pallas kernels: 5.66 us -> 4.12 us  [shards(): pl.pallas_call(functools.partial(survive_kernel, bins, slots, window), gr...]
  transfers between devices with their start and end apart: 3 -> 3, of which waited for: 2 -> 3; matrix products, arithmetic and copies ran while one was open for 1% -> 1% of each run, Pallas kernels for 9% -> 10%
where the time goes in v3:
time: 71.4 us; the launch traced here: 70.9 us
  Pallas kernels  34.3 us (48%)
  waiting for transfers between devices  23.6 us (33%)
  starting transfers between devices  10.2 us (14%)
  local copies, waits for them, and re-layouts  1.59 us (2%)
    all_to_all x2, waiting for transfers between devices, exchange(): lax.all_to_all(message, axes, split_axis=0, concat_axis=0, tiled=True)  23 us
    pallas_call x1, Pallas kernels, shards(): pl.pallas_call(functools.partial(river_kernel, slots), out_shape=(jax.Sha...  18.9 us
    all_to_all x2, starting transfers between devices, exchange(): lax.all_to_all(message, axes, split_axis=0, concat_axis=0, tiled=True)  9.92 us
    pallas_call x1, Pallas kernels, shards(): pl.pallas_call(functools.partial(transit_kernel, kinds, bins), out_shape=...  7.28 us
    pallas_call x1, Pallas kernels, shards(): pl.pallas_call(functools.partial(survive_kernel, bins, slots, window), gr...  4.12 us
    pallas_call x1, Pallas kernels, shards(): pl.pallas_call(functools.partial(rain_kernel, bins, slots), grid=(patches...  4.01 us
    unnamed x6, local copies, waits for them, and re-layouts  1.59 us
  transfers between devices with their start and end apart: 3, of which 3 were waited for; matrix products, arithmetic and copies ran while one was open for 1% of the time, Pallas kernels for 10%

profile of v3, /device:TPU:0, one launch (start us, length us, event | category | flops | bytes accessed | tf_op | source)
XLA Modules:
  0.0 70.9 jit_solution(4602844960822875642)
XLA Ops:
  0.6 4.0 %rain.1 = (f32[1344,128]{1,0:T(8,128)}, f32[56,128]{1,0:T(8,128)}) custom-call(s32[1]{0:T(128)} %bitcast.1.core_ref, f32[4,64]{1,0:T(4,128)} %trait_ref.5, f32[3072,128]{1,0:T(8,128)} %bitcast.15, f32[48,128]{1,0:T(8,128)} %area_ref.1, f32[5,128]{1,0:T(8,128)} %force_ref.3, s32[8,128]{1,0:T(8,128)} %bitcast.24, f32[8,128]{1,0:T(8,128)} %bitcast.26, ...), custom_call_target="tpu_custom_call" | custom-call | tf_op jit(solution)/shard_map/rain/pallas_call | solution.py:500
  4.7 7.3 %all-to-all-start = ((f32[32,21,2,128]{3,2,1,0:T(2,128)}), f32[32,21,2,128]{3,2,1,0:T(2,128)S(1)}, u32[]{:S(2)}, u32[]{:S(2)}) async-start(f32[32,21,2,128]{3,2,1,0:T(2,128)} %bitcast.19), calls=%async_computation | async-start | bytes 1376256 | tf_op jit(solution)/shard_map/all_to_all | solution.py:494
  12.0 0.3 collective-permute-start
  12.3 0.6 pad_add_fusion.here_ref
  12.9 0.5 collective-permute-done.mate_ref
  13.5 0.0 copy-start.2
  13.5 18.3 %all-to-all-done = f32[32,21,2,128]{3,2,1,0:T(2,128)S(1)} async-done(((f32[32,21,2,128]{3,2,1,0:T(2,128)}), f32[32,21,2,128]{3,2,1,0:T(2,128)S(1)}, u32[]{:S(2)}, u32[]{:S(2)}) %all-to-all-start) | async-done | bytes 688160 | tf_op jit(solution)/shard_map/all_to_all | solution.py:494
  31.7 0.0 copy-start
  31.7 0.0 copy-done.2
  31.7 0.8 %copy-done = f32[32,21,2,128]{3,2,1,0:T(2,128)} copy-done((f32[32,21,2,128]{3,2,1,0:T(2,128)}, f32[32,21,2,128]{3,2,1,0:T(2,128)S(1)}, u32[]{:S(2)}) %copy-start) | copy-done | bytes 688152
  32.6 18.9 %river.1 = (f32[640,128]{1,0:T(8,128)}, f32[2,16,128]{2,1,0:T(8,128)}, f32[32,128]{1,0:T(8,128)}) custom-call(s32[2]{0:T(128)} %pad_add_fusion.here_ref, f32[1344,128]{1,0:T(8,128)} %bitcast.17, s32[8,128]{1,0:T(8,128)} %bitcast.23, f32[56,128]{1,0:T(8,128)} %copy-done.2, f32[4,2048]{1,0:T(4,128)} %water_ref.3, f32[4,2048]{1,0:T(4,128)} %rate_ref.3), custom_call_target="tpu_custom_call" | custom-call | tf_op jit(solution)/shard_map/river/pallas_call | solution.py:552
  51.5 2.6 %all-to-all-start.1 = ((f32[32,5,4,128]{3,2,1,0:T(4,128)}), f32[32,5,4,128]{3,2,1,0:T(4,128)S(1)}, u32[]{:S(2)}, u32[]{:S(2)}) async-start(f32[32,5,4,128]{3,2,1,0:T(4,128)} %bitcast.20), calls=%async_computation.1 | async-start | bytes 655360 | tf_op jit(solution)/shard_map/all_to_all | solution.py:494
  54.1 7.3 %transit.1.moved_ref = f32[3072,128]{1,0:T(8,128)} custom-call(f32[4,64]{1,0:T(4,128)} %trait_ref.5, f32[192,48]{1,0:T(8,128)} %bitcast.21, f32[3072,128]{1,0:T(8,128)} %bitcast.16, f32[5,128]{1,0:T(8,128)} %force_ref.3, f32[4,128]{1,0:T(4,128)} %weight_ref.1), custom_call_target="tpu_custom_call" | custom-call | tf_op jit(solution)/shard_map/transit/pallas_call | solution.py:541
  61.3 4.7 %all-to-all-done.1 = f32[32,5,4,128]{3,2,1,0:T(4,128)S(1)} async-done(((f32[32,5,4,128]{3,2,1,0:T(4,128)}), f32[32,5,4,128]{3,2,1,0:T(4,128)S(1)}, u32[]{:S(2)}, u32[]{:S(2)}) %all-to-all-start.1) | async-done | bytes 327712 | tf_op jit(solution)/shard_map/all_to_all | solution.py:494
  66.1 0.0 copy-start.1
  66.1 0.7 %copy-done.1 = f32[32,5,4,128]{3,2,1,0:T(4,128)} copy-done((f32[32,5,4,128]{3,2,1,0:T(4,128)}, f32[32,5,4,128]{3,2,1,0:T(4,128)S(1)}, u32[]{:S(2)}) %copy-start.1) | copy-done | bytes 327704
  66.8 4.1 %survive.1 = (f32[3072,128]{1,0:T(8,128)}, f32[1,128]{1,0:T(1,128)}, f32[4,2048]{1,0:T(4,128)}) custom-call(s32[2]{0:T(128)} %pad_add_fusion.here_ref, f32[4,64]{1,0:T(4,128)} %trait_ref.5, f32[640,128]{1,0:T(8,128)} %bitcast.18, f32[2,16,128]{2,1,0:T(8,128)} %get-tuple-element.14.hill_ref, f32[32,128]{1,0:T(8,128)} %get-tuple-element.15.room_ref, ...), custom_call_target="tpu_custom_call" | custom-call | tf_op jit(solution)/shard_map/survive/pallas_call | solution.py:578
Async XLA Ops:
  4.7 27.1 %all-to-all-start = ((f32[32,21,2,128]{3,2,1,0:T(2,128)}), f32[32,21,2,128]{3,2,1,0:T(2,128)S(1)}, u32[]{:S(2)}, u32[]{:S(2)}) async-start(f32[32,21,2,128]{3,2,1,0:T(2,128)} %bitcast.19), calls=%async_computation | async-start | bytes 1376256 | tf_op jit(solution)/shard_map/all_to_all | solution.py:494
  12.0 1.5 %collective-permute-start = (f32[56,128]{1,0:T(8,128)}, f32[56,128]{1,0:T(8,128)S(1)}, u32[]{:S(2)}, u32[]{:S(2)}) collective-permute-start(f32[56,128]{1,0:T(8,128)} %get-tuple-element.12), channel_id=1, source_target_pairs={{0,1},{1,0},{2,3},{3,2},{4,5},{5,4},{6,7},{7,6},{8,9},{9,8},{10,11... | collective-permute-start | bytes 86024 | tf_op jit(solution)/shard_map/ppermute | solution.py:539
  13.5 18.3 %copy-start.2 = (f32[56,128]{1,0:T(8,128)}, f32[56,128]{1,0:T(8,128)S(1)}, u32[]{:S(2)}) copy-start(f32[56,128]{1,0:T(8,128)S(1)} %collective-permute-done.mate_ref) | copy-start | bytes 86020
  31.7 0.8 %copy-start = (f32[32,21,2,128]{3,2,1,0:T(2,128)}, f32[32,21,2,128]{3,2,1,0:T(2,128)S(1)}, u32[]{:S(2)}) copy-start(f32[32,21,2,128]{3,2,1,0:T(2,128)S(1)} %all-to-all-done) | copy-start | bytes 2064388
  51.5 14.6 %all-to-all-start.1 = ((f32[32,5,4,128]{3,2,1,0:T(4,128)}), f32[32,5,4,128]{3,2,1,0:T(4,128)S(1)}, u32[]{:S(2)}, u32[]{:S(2)}) async-start(f32[32,5,4,128]{3,2,1,0:T(4,128)} %bitcast.20), calls=%async_computation.1 | async-start | bytes 655360 | tf_op jit(solution)/shard_map/all_to_all | solution.py:494
  66.1 0.7 %copy-start.1 = (f32[32,5,4,128]{3,2,1,0:T(4,128)}, f32[32,5,4,128]{3,2,1,0:T(4,128)S(1)}, u32[]{:S(2)}) copy-start(f32[32,5,4,128]{3,2,1,0:T(4,128)S(1)} %all-to-all-done.1) | copy-start | bytes 983044

commit v4 on v3

--- a/solution.py
+++ b/solution.py
@@ -11,13 +11,16 @@
 
 NSUB = 12
 LANES = 128
-PHASE = 2
 F32 = jnp.float32
 BF16 = jnp.bfloat16
 
 VMEM = pl.BlockSpec(memory_space=pltpu.VMEM)
 ANY = pl.BlockSpec(memory_space=pl.ANY)
 SMEM = pl.BlockSpec(memory_space=pltpu.SMEM)
+
+
+def on_chip(value):
+    return pltpu.with_memory_space_constraint(value, pltpu.VMEM)
 
 
 def lane_iota(shape):
@@ -220,10 +223,10 @@
     out_ref,
     hill_out_ref,
     room_ref,
-    lo_ref,
-    mask_ref,
+    lo_refs,
+    mask_refs,
+    speed_refs,
     state_ref,
-    speed_ref,
     value_ref,
     rows_left_ref,
     rows_lo_ref,
@@ -236,7 +239,7 @@
     size = 2 * chunks + rows + 2
     peers = arrived_ref.shape[0] // size
     spans = 2 * chunks
-    window = state_ref.shape[0]
+    window = NSUB + 2
     base = here_ref[0]
     core = here_ref[1]
     other = 1 - core
@@ -246,37 +249,45 @@
         return jnp.where(j >= peers, j - peers, j)
 
     square = (LANES, LANES)
+    lane = lane_iota(square).astype(F32)
     eye = jnp.where(row_iota(square) == lane_iota(square), 1.0, 0.0).astype(BF16)
     wide = (2 * LANES, 2 * LANES)
     ones = jnp.where(row_iota(wide) // LANES == lane_iota(wide) // LANES, 1.0, 0.0).astype(BF16)
-    lane = lane_iota(square).astype(F32)
-
-    def table(b, carry):
-        j = block_of(b)
+
+    def table(pair, at):
+        j = block_of(2 * pair + at)
         target = arrived_ref[pl.ds(j * size, chunks), :].astype(jnp.int32)
         span = target >> 7
         low = (target & 127).astype(F32)
-        for h in range(0, chunks, 2):
-            diagonal = jnp.concatenate(
-                [
-                    jnp.broadcast_to(low[h + i : h + i + 1, :], square).astype(BF16) * eye
-                    for i in range(2)
-                ],
-                axis=1,
-            )
-            column = jnp.dot(diagonal, ones, preferred_element_type=F32)
-            for i in range(2):
-                at = slice((h + i) * LANES, (h + i + 1) * LANES)
-                mask_ref[b, h + i] = jnp.where(
-                    row_iota((spans, LANES)) == span[h + i : h + i + 1, :], 1.0, 0.0
-                ).astype(BF16)
-                lo_ref[b, at, :] = jnp.where(
-                    column[:, i * LANES : (i + 1) * LANES] == lane, 1.0, 0.0
-                ).astype(BF16)
-        speed_ref[b] = arrived_ref[pl.ds(j * size + chunks, chunks), :]
-        return carry
-
-    lax.fori_loop(0, window - 1, table, 0)
+        half = chunks // 2
+        diagonal = jnp.concatenate(
+            [
+                jnp.concatenate(
+                    [
+                        jnp.broadcast_to(low[h + i * half : h + i * half + 1, :], square).astype(BF16)
+                        * eye
+                        for h in range(half)
+                    ],
+                    axis=0,
+                )
+                for i in range(2)
+            ],
+            axis=1,
+        )
+        columns = jnp.dot(diagonal, ones, preferred_element_type=F32)
+        for h in range(chunks):
+            i, k = divmod(h, half)
+            column = columns[k * LANES : (k + 1) * LANES, i * LANES : (i + 1) * LANES]
+            mask_refs[pair][at, h] = jnp.where(
+                row_iota((spans, LANES)) == span[h : h + 1, :], 1.0, 0.0
+            ).astype(BF16)
+            lo_refs[pair][at, h * LANES : (h + 1) * LANES, :] = jnp.where(
+                column == lane, 1.0, 0.0
+            ).astype(BF16)
+        speed_refs[pair][at] = arrived_ref[pl.ds(j * size + chunks, chunks), :]
+
+    table(0, 0)
+    table(0, 1)
 
     fraction = 1.0 / NSUB
     half = 3 * chunks
@@ -321,47 +332,63 @@
     deep = [jnp.where(core == 0, runoff_ref[which, 2], 0.0) for which in range(2)]
     surface = [runoff_ref[0, 0], runoff_ref[0, 1], runoff_ref[1, core]]
 
-    def block_flow(b):
-        out = speed_ref[b] * state_ref[b]
-        high, low = split2(out)
-        value_ref[b, 0] = high
-        value_ref[b, 1] = low
+    def pair_flow(pair):
+        outs = []
+        for i in range(2):
+            out = speed_refs[pair][i] * state_ref[2 * pair + i]
+            high, low = split2(out)
+            value_ref[pair, 2 * i] = high
+            value_ref[pair, 2 * i + 1] = low
+            outs.append(out)
         pieces = []
         for h in range(chunks):
-            mask = mask_ref[b, h]
+            masks = [mask_refs[pair][i, h] for i in range(2)]
             pieces.append(
                 jnp.concatenate(
                     [
-                        jnp.broadcast_to(value_ref[b, s, h : h + 1, :], (spans, LANES)).astype(BF16)
-                        * mask
-                        for s in range(2)
+                        jnp.broadcast_to(value_ref[pair, m, h : h + 1, :], (spans, LANES)).astype(BF16)
+                        * masks[m // 2]
+                        for m in range(4)
                     ],
                     axis=0,
                 )
             )
         flow = jnp.dot(
-            jnp.concatenate(pieces, axis=1), lo_ref[b], preferred_element_type=F32
+            jnp.concatenate(pieces, axis=1),
+            jnp.concatenate([lo_refs[pair][0], lo_refs[pair][1]], axis=1),
+            preferred_element_type=F32,
         )
-        return out, flow[0:spans] + flow[spans : 2 * spans]
-
-    def advance(count):
-        for b in reversed(range(count)):
-            out, flow = block_flow(b)
-            state_ref[b] = state_ref[b] - out + flow[0:chunks]
-            state_ref[b + 1] += flow[chunks:spans]
-
-    for phase in range(NSUB // PHASE):
-
-        def step(t, carry):
-            advance(phase * PHASE + PHASE + 1)
-            gone = [hill_rate_ref[i] * hill_ref[i] for i in range(3)]
-            for i in range(3):
-                hill_ref[i] = hill_ref[i] - gone[i] + surface[i]
-            state_ref[core] += jnp.where(core == 0, gone[0], gone[1]) + deep[0]
-            state_ref[other] += gone[2] + deep[1]
+        flows = []
+        for i in range(2):
+            part = flow[2 * i * spans : 2 * (i + 1) * spans, i * LANES : (i + 1) * LANES]
+            flows.append(part[0:spans] + part[spans:])
+        return outs, flows
+
+    def advance(pairs):
+        for pair in reversed(range(pairs)):
+            outs, flows = pair_flow(pair)
+            b = 2 * pair
+            state_ref[b + 2] += flows[1][chunks:]
+            state_ref[b + 1] = state_ref[b + 1] - outs[1] + flows[1][:chunks] + flows[0][chunks:]
+            state_ref[b] = state_ref[b] - outs[0] + flows[0][:chunks]
+        gone = [hill_rate_ref[i] * hill_ref[i] for i in range(3)]
+        for i in range(3):
+            hill_ref[i] = hill_ref[i] - gone[i] + surface[i]
+        state_ref[core] += jnp.where(core == 0, gone[0], gone[1]) + deep[0]
+        state_ref[other] += gone[2] + deep[1]
+
+    table(1, 0)
+    table(1, 1)
+    advance(1)
+    for pairs in range(2, NSUB // 2 + 1):
+
+        def step(i, carry):
+            table(pairs, i)
+            advance(pairs)
             return carry
 
-        lax.fori_loop(0, PHASE, step, 0)
+        lax.fori_loop(0, 2, step, 0)
+    advance(NSUB // 2 + 1)
 
     hill_out_ref[...] = hill_ref[0:2]
 
@@ -450,9 +477,10 @@
             alive_ref[k : k + 1, :] = jnp.exp(-trait_ref[3, k] * flooded)
 
     alive = alive_ref[...]
-    for p in range(moved_ref.shape[0] // bins):
-        at = slice(p * bins, (p + 1) * bins)
-        out_ref[at, :] = moved_ref[at, :] * alive
+    base = pl.program_id(0) * out_ref.shape[0]
+    for p in range(out_ref.shape[0] // bins):
+        at = pl.ds(pl.multiple_of(base + p * bins, bins), bins)
+        out_ref[p * bins : (p + 1) * bins, :] = moved_ref[at, :] * alive
 
 
 def shards(
@@ -492,7 +520,7 @@
         inner = math.gcd(size, 8)
         message = message.reshape(peers, size // inner, inner, LANES)
         arrived = lax.all_to_all(message, axes, split_axis=0, concat_axis=0, tiled=True)
-        return arrived.reshape(peers * size, LANES)
+        return on_chip(arrived.reshape(peers * size, LANES))
 
     size = 2 * chunks + rows + 2
     tile = 16
@@ -501,8 +529,8 @@
         functools.partial(rain_kernel, bins, slots),
         grid=(patches // tile,),
         out_shape=(
-            jax.ShapeDtypeStruct((peers * size, LANES), F32),
-            jax.ShapeDtypeStruct((3 * chunks + rows, LANES), F32),
+            pltpu.VMEM((peers * size, LANES), F32),
+            pltpu.VMEM((3 * chunks + rows, LANES), F32),
         ),
         in_specs=[
             SMEM,
@@ -520,6 +548,7 @@
         ],
         out_specs=(whole(peers * size, LANES), whole(3 * chunks + rows, LANES)),
         scratch_shapes=[pltpu.VMEM((1, LANES), F32)],
+        compiler_params=pltpu.CompilerParams(vmem_limit_bytes=16 << 20),
         name="rain",
     )(
         here[1:2],
@@ -536,14 +565,15 @@
         capacity.reshape(chunks, LANES),
     )
     arrived = exchange(message, size)
-    mate = lax.ppermute(mate, axes, [(i, i + 1 - 2 * (i % 2)) for i in range(peers)])
+    mate = on_chip(lax.ppermute(mate, axes, [(i, i + 1 - 2 * (i % 2)) for i in range(peers)]))
 
     moved = pl.pallas_call(
         functools.partial(transit_kernel, kinds, bins),
-        out_shape=jax.ShapeDtypeStruct((patches * bins, LANES), F32),
+        out_shape=pltpu.VMEM((patches * bins, LANES), F32),
         in_specs=[SMEM, VMEM, VMEM, VMEM, VMEM],
         out_specs=VMEM,
         scratch_shapes=[pltpu.VMEM((kinds * patches, 3 * patches), BF16)],
+        compiler_params=pltpu.CompilerParams(vmem_limit_bytes=16 << 20),
         name="transit",
     )(cohort_traits, transitions.reshape(kinds * patches, patches), bio, cell_forcing, disturb_weight)
 
@@ -552,24 +582,25 @@
     parts, hill, room = pl.pallas_call(
         functools.partial(river_kernel, slots),
         out_shape=(
-            jax.ShapeDtypeStruct((peers * out_size, LANES), F32),
-            jax.ShapeDtypeStruct((2, chunks, LANES), F32),
-            jax.ShapeDtypeStruct((peers, LANES), F32),
+            pltpu.VMEM((peers * out_size, LANES), F32),
+            pltpu.VMEM((2, chunks, LANES), F32),
+            pltpu.VMEM((peers, LANES), F32),
         ),
         in_specs=[SMEM] + [VMEM] * 5,
         out_specs=(VMEM, VMEM, VMEM),
         scratch_shapes=[
-            pltpu.VMEM((window - 1, rivers, LANES), BF16),
-            pltpu.VMEM((window - 1, chunks, spans, LANES), BF16),
-            pltpu.VMEM((window, chunks, LANES), F32),
-            pltpu.VMEM((window - 1, chunks, LANES), F32),
-            pltpu.VMEM((window - 1, 2, chunks, LANES), F32),
+            [pltpu.VMEM((2, rivers, LANES), BF16)] * (window // 2),
+            [pltpu.VMEM((2, chunks, spans, LANES), BF16)] * (window // 2),
+            [pltpu.VMEM((2, chunks, LANES), F32)] * (window // 2),
+            pltpu.VMEM((window + 1, chunks, LANES), F32),
+            pltpu.VMEM((window // 2, 4, chunks, LANES), F32),
             pltpu.VMEM((2, rows, 6 * chunks, LANES), BF16),
             pltpu.VMEM((2, rows, LANES, LANES), BF16),
             pltpu.VMEM((3, chunks, LANES), F32),
             pltpu.VMEM((3, chunks, LANES), F32),
             pltpu.VMEM((2, 3, chunks, LANES), F32),
         ],
+        compiler_params=pltpu.CompilerParams(vmem_limit_bytes=32 << 20),
         name="river",
     )(here, arrived, target, mate, river_water, river_rates)
     parts = exchange(parts, out_size)
@@ -586,12 +617,12 @@
         in_specs=[
             SMEM,
             SMEM,
-            whole(peers * out_size, LANES),
-            whole(2, chunks, LANES),
-            whole(peers, LANES),
+            VMEM,
+            VMEM,
+            VMEM,
             whole(rows, LANES),
             whole(rows, LANES),
-            pl.BlockSpec((tile * bins, LANES), lambda i: (i, 0)),
+            VMEM,
         ],
         out_specs=(
             pl.BlockSpec((tile * bins, LANES), lambda i: (i, 0)),
@@ -599,8 +630,9 @@
             whole(4, rivers),
         ),
         scratch_shapes=[pltpu.VMEM((bins, LANES), F32), pltpu.VMEM((peers, LANES), F32)],
+        compiler_params=pltpu.CompilerParams(vmem_limit_bytes=16 << 20),
         name="survive",
-    )(here, cohort_traits, parts, hill, room, share, source, moved)
+    )(here, cohort_traits, parts, on_chip(hill), on_chip(room), share, source, on_chip(moved))
     return (new_biomass.reshape(patches, bins, lands), flooded.reshape(lands), river_state)
 
 

time: 71.4 us -> 71.5 us (level)
  Pallas kernels: 34.3 us -> 25.1 us
  local copies, waits for them, and re-layouts: 1.59 us -> 9.4 us
  waiting for transfers between devices: 23.6 us -> 25.2 us
    unnamed x6 -> x42, local copies, waits for them, and re-layouts: 1.59 us -> 9.4 us
    pallas_call x1, Pallas kernels: 18.9 us -> 14.4 us  [shards(): pl.pallas_call(functools.partial(river_kernel, slots), out_shape=(pltpu.V...]
    pallas_call x1, Pallas kernels: 7.28 us -> 5.2 us  [shards(): pl.pallas_call(functools.partial(transit_kernel, kinds, bins), out_shape=...]
    pallas_call x1, Pallas kernels: 4.12 us -> 2.7 us  [shards(): pl.pallas_call(functools.partial(survive_kernel, bins, slots, window), gr...]
    all_to_all x2, waiting for transfers between devices: 23 us -> 24.3 us  [exchange(): lax.all_to_all(message, axes, split_axis=0, concat_axis=0, tiled=True)]
    pallas_call x1, Pallas kernels: 4.01 us -> 2.83 us  [shards(): pl.pallas_call(functools.partial(rain_kernel, bins, slots), grid=(patches...]
  transfers between devices with their start and end apart: 3 -> 3, of which waited for: 3 -> 3; matrix products, arithmetic and copies ran while one was open for 1% -> 0% of each run, Pallas kernels for 10% -> 7%
where the time goes in v4:
time: 71.5 us; the launch traced here: 70.8 us
  waiting for transfers between devices  25.2 us (35%)
  Pallas kernels  25.1 us (35%)
  starting transfers between devices  10.2 us (14%)
  local copies, waits for them, and re-layouts  9.4 us (13%)
  between operations  0.76 us (1%)
    all_to_all x2, waiting for transfers between devices, exchange(): lax.all_to_all(message, axes, split_axis=0, concat_axis=0, tiled=True)  24.3 us
    pallas_call x1, Pallas kernels, shards(): pl.pallas_call(functools.partial(river_kernel, slots), out_shape=(pltpu.V...  14.4 us
    all_to_all x2, starting transfers between devices, exchange(): lax.all_to_all(message, axes, split_axis=0, concat_axis=0, tiled=True)  9.92 us
    unnamed x42, local copies, waits for them, and re-layouts  9.4 us
    pallas_call x1, Pallas kernels, shards(): pl.pallas_call(functools.partial(transit_kernel, kinds, bins), out_shape=...  5.2 us
    pallas_call x1, Pallas kernels, shards(): pl.pallas_call(functools.partial(rain_kernel, bins, slots), grid=(patches...  2.83 us
    pallas_call x1, Pallas kernels, shards(): pl.pallas_call(functools.partial(survive_kernel, bins, slots, window), gr...  2.7 us
  transfers between devices with their start and end apart: 3, of which 3 were waited for; matrix products, arithmetic and copies ran while one was open for 0% of the time, Pallas kernels for 7%

profile of v4, /device:TPU:0, one launch (start us, length us, event | category | flops | bytes accessed | tf_op | source)
XLA Modules:
  0.0 70.8 jit_solution(3497769902457407749)
XLA Ops:
  0.6 0.0 copy-start.3
  0.6 0.0 copy-start.11
  0.7 0.0 copy-start
  0.7 1.4 %copy-done = f32[48,64,128]{2,1,0:T(8,128)S(1)} copy-done((f32[48,64,128]{2,1,0:T(8,128)S(1)}, f32[48,64,128]{2,1,0:T(8,128)}, u32[]{:S(2)}) %copy-start) | copy-done | bytes 1572888
  2.1 0.8 %copy-done.2 = f32[4,2048]{1,0:T(4,128)S(1)} copy-done((f32[4,2048]{1,0:T(4,128)S(1)}, f32[4,2048]{1,0:T(4,128)}, u32[]{:S(2)}) %copy-start.2) | copy-done | bytes 32792
  2.8 0.8 %copy-done.4 = f32[4,2048]{1,0:T(4,128)S(1)} copy-done((f32[4,2048]{1,0:T(4,128)S(1)}, f32[4,2048]{1,0:T(4,128)}, u32[]{:S(2)}) %copy-start.4) | copy-done | bytes 32792
  3.6 0.7 %copy-done.7 = f32[48,128]{1,0:T(8,128)S(1)} copy-done((f32[48,128]{1,0:T(8,128)S(1)}, f32[48,128]{1,0:T(8,128)}, u32[]{:S(2)}) %copy-start.7) | copy-done | bytes 24600
  4.3 0.7 copy-done.8
  5.0 0.7 copy-done.10
  5.7 0.7 copy-done.12
  6.4 0.7 copy-done.14
  7.1 0.7 copy-done.16
  7.8 0.7 copy-done.18
  8.5 0.7 copy-done.19
  9.2 2.8 %rain.1 = (f32[1344,128]{1,0:T(8,128)}, f32[56,128]{1,0:T(8,128)S(1)}) custom-call(s32[1]{0:T(128)} %bitcast.1.core_ref, f32[4,64]{1,0:T(4,128)S(1)} %copy-done.8, f32[3072,128]{1,0:T(8,128)S(1)} %bitcast.15, f32[48,128]{1,0:T(8,128)S(1)} %copy-done.7, f32[5,128]{1,0:T(8,128)S(1)} %copy-done.12, s32[8,128]{1,0:T(8,128)S(1)} %bitcast.22, ...), custom_call_target="tpu_custom_call" | custom-call | tf_op jit(solution)/shard_map/rain/pallas_call | solution.py:528
  12.0 7.3 %all-to-all-start = ((f32[32,21,2,128]{3,2,1,0:T(2,128)}), f32[32,21,2,128]{3,2,1,0:T(2,128)S(1)}, u32[]{:S(2)}, u32[]{:S(2)}) async-start(f32[32,21,2,128]{3,2,1,0:T(2,128)} %bitcast.8), calls=%async_computation | async-start | bytes 1376256 | tf_op jit(solution)/shard_map/all_to_all | solution.py:522
  19.3 0.3 collective-permute-start
  19.7 0.1 pad_add_fusion.here_ref
  19.7 0.9 %collective-permute-done.mate_ref = f32[56,128]{1,0:T(8,128)S(1)} collective-permute-done((f32[56,128]{1,0:T(8,128)S(1)}, f32[56,128]{1,0:T(8,128)S(1)}, u32[]{:S(2)}, u32[]{:S(2)}) %collective-permute-start) | collective-permute-done | bytes 28704 | tf_op jit(solution)/shard_map/ppermute | solution.py:568
  20.6 18.5 %all-to-all-done = f32[32,21,2,128]{3,2,1,0:T(2,128)S(1)} async-done(((f32[32,21,2,128]{3,2,1,0:T(2,128)}), f32[32,21,2,128]{3,2,1,0:T(2,128)S(1)}, u32[]{:S(2)}, u32[]{:S(2)}) %all-to-all-start) | async-done | bytes 688160 | tf_op jit(solution)/shard_map/all_to_all | solution.py:522
  39.1 0.0 copy-done.3
  39.1 0.0 copy-done.11
  39.1 0.0 copy-done.5
  39.1 14.4 %river.1 = (f32[640,128]{1,0:T(8,128)}, f32[2,16,128]{2,1,0:T(8,128)S(1)}, f32[32,128]{1,0:T(8,128)S(1)}) custom-call(s32[2]{0:T(128)S(1)} %pad_add_fusion.here_ref, f32[1344,128]{1,0:T(8,128)S(1)} %bitcast.17, s32[8,128]{1,0:T(8,128)S(1)} %bitcast.21, f32[56,128]{1,0:T(8,128)S(1)} %collective-permute-done.mate_ref, f32[4,2048]{1,0:T(4,128)S(1)} %copy-done.3, ...), custom_call_target="tpu_custom_call" | custom-call | tf_op jit(solution)/shard_map/river/pallas_call | solution.py:582
  53.5 2.6 %all-to-all-start.1 = ((f32[32,5,4,128]{3,2,1,0:T(4,128)}), f32[32,5,4,128]{3,2,1,0:T(4,128)S(1)}, u32[]{:S(2)}, u32[]{:S(2)}) async-start(f32[32,5,4,128]{3,2,1,0:T(4,128)} %bitcast.10), calls=%async_computation.1 | async-start | bytes 655360 | tf_op jit(solution)/shard_map/all_to_all | solution.py:522
  56.1 0.0 copy-done.1
  56.1 0.0 copy-done.9
  56.1 0.0 copy-start.6
  56.1 0.9 %copy-done.6 = f32[4,48,48]{2,1,0:T(8,128)S(1)} copy-done((f32[4,48,48]{2,1,0:T(8,128)S(1)}, f32[4,48,48]{2,1,0:T(8,128)}, u32[]{:S(2)}) %copy-start.6) | copy-done | bytes 36888
  57.0 5.2 %transit.1.moved_ref = f32[3072,128]{1,0:T(8,128)S(1)} custom-call(f32[4,64]{1,0:T(4,128)S(1)} %copy-done.9, f32[192,48]{1,0:T(8,128)S(1)} %bitcast.19, f32[3072,128]{1,0:T(8,128)S(1)} %bitcast.16, f32[5,128]{1,0:T(8,128)S(1)} %copy-done.13, f32[4,128]{1,0:T(4,128)S(1)} %copy-done.20), custom_call_target="tpu_custom_call" | custom-call | tf_op jit(solution)/shard_map/transit/pallas_call | solution.py:570
  62.2 5.9 %all-to-all-done.1 = f32[32,5,4,128]{3,2,1,0:T(4,128)S(1)} async-done(((f32[32,5,4,128]{3,2,1,0:T(4,128)}), f32[32,5,4,128]{3,2,1,0:T(4,128)S(1)}, u32[]{:S(2)}, u32[]{:S(2)}) %all-to-all-start.1) | async-done | bytes 327712 | tf_op jit(solution)/shard_map/all_to_all | solution.py:522
  68.1 2.7 %survive.1 = (f32[3072,128]{1,0:T(8,128)}, f32[1,128]{1,0:T(1,128)}, f32[4,2048]{1,0:T(4,128)}) custom-call(s32[2]{0:T(128)S(1)} %pad_add_fusion.here_ref, f32[4,64]{1,0:T(4,128)S(1)} %copy-done.9, f32[640,128]{1,0:T(8,128)S(1)} %bitcast.18, f32[2,16,128]{2,1,0:T(8,128)S(1)} %get-tuple-element.14.hill_ref, f32[32,128]{1,0:T(8,128)S(1)} %get-tuple-element.15.room_ref, ...), custom_call_target="tpu_custom_call" | custom-call | tf_op jit(solution)/shard_map/survive/pallas_call | solution.py:609
  (21 shorter events, 0.0 us)
Async XLA Ops:
  0.6 38.5 %copy-start.3 = (f32[4,2048]{1,0:T(4,128)S(1)}, f32[4,2048]{1,0:T(4,128)}, u32[]{:S(2)}) copy-start(f32[4,2048]{1,0:T(4,128)} %water_ref.3) | copy-start | bytes 98308
  0.6 38.5 %copy-start.11 = (s32[1024]{0:T(1024)S(1)}, s32[1024]{0:T(1024)}, u32[]{:S(2)}) copy-start(s32[1024]{0:T(1024)} %param.21) | copy-start | bytes 12292
  0.7 1.4 %copy-start = (f32[48,64,128]{2,1,0:T(8,128)S(1)}, f32[48,64,128]{2,1,0:T(8,128)}, u32[]{:S(2)}) copy-start(f32[48,64,128]{2,1,0:T(8,128)} %param.13) | copy-start | bytes 4718596
  2.1 0.8 %copy-start.2 = (f32[4,2048]{1,0:T(4,128)S(1)}, f32[4,2048]{1,0:T(4,128)}, u32[]{:S(2)}) copy-start(f32[4,2048]{1,0:T(4,128)} %water_ref.3) | copy-start | bytes 98308
  2.8 0.8 %copy-start.4 = (f32[4,2048]{1,0:T(4,128)S(1)}, f32[4,2048]{1,0:T(4,128)}, u32[]{:S(2)}) copy-start(f32[4,2048]{1,0:T(4,128)} %rate_ref.3) | copy-start | bytes 98308
  3.6 0.7 %copy-start.7 = (f32[48,128]{1,0:T(8,128)S(1)}, f32[48,128]{1,0:T(8,128)}, u32[]{:S(2)}) copy-start(f32[48,128]{1,0:T(8,128)} %area_ref.1) | copy-start | bytes 73732
  4.3 0.7 copy-start.8
  5.0 0.7 copy-start.10
  5.7 0.7 copy-start.12
  6.4 0.7 copy-start.14
  7.1 0.7 copy-start.16
  7.8 0.7 copy-start.18
  8.5 0.7 copy-start.19
  9.2 29.9 %copy-start.5 = (f32[4,2048]{1,0:T(4,128)S(1)}, f32[4,2048]{1,0:T(4,128)}, u32[]{:S(2)}) copy-start(f32[4,2048]{1,0:T(4,128)} %rate_ref.3) | copy-start | bytes 98308
  12.0 44.1 %copy-start.1 = (f32[48,64,128]{2,1,0:T(8,128)S(1)}, f32[48,64,128]{2,1,0:T(8,128)}, u32[]{:S(2)}) copy-start(f32[48,64,128]{2,1,0:T(8,128)} %param.13) | copy-start | bytes 4718596
  12.0 44.1 %copy-start.9 = (f32[4,64]{1,0:T(4,128)S(1)}, f32[4,64]{1,0:T(4,128)}, u32[]{:S(2)}) copy-start(f32[4,64]{1,0:T(4,128)} %trait_ref.5) | copy-start | bytes 3076
  12.0 44.1 %copy-start.13 = (f32[5,128]{1,0:T(8,128)S(1)}, f32[5,128]{1,0:T(8,128)}, u32[]{:S(2)}) copy-start(f32[5,128]{1,0:T(8,128)} %force_ref.3) | copy-start | bytes 7684
  12.0 44.1 %copy-start.20 = (f32[4,128]{1,0:T(4,128)S(1)}, f32[4,128]{1,0:T(4,128)}, u32[]{:S(2)}) copy-start(f32[4,128]{1,0:T(4,128)} %weight_ref.1) | copy-start | bytes 6148
  12.0 27.1 %all-to-all-start = ((f32[32,21,2,128]{3,2,1,0:T(2,128)}), f32[32,21,2,128]{3,2,1,0:T(2,128)S(1)}, u32[]{:S(2)}, u32[]{:S(2)}) async-start(f32[32,21,2,128]{3,2,1,0:T(2,128)} %bitcast.8), calls=%async_computation | async-start | bytes 1376256 | tf_op jit(solution)/shard_map/all_to_all | solution.py:522
  19.3 1.3 %collective-permute-start = (f32[56,128]{1,0:T(8,128)S(1)}, f32[56,128]{1,0:T(8,128)S(1)}, u32[]{:S(2)}, u32[]{:S(2)}) collective-permute-start(f32[56,128]{1,0:T(8,128)S(1)} %get-tuple-element.12), channel_id=1, source_target_pairs={{0,1},{1,0},{2,3},{3,2},{4,5},{5,4},{6,7},{7,6},{8,9},{9,8},{10,11... | collective-permute-start | bytes 86024 | tf_op jit(solution)/shard_map/ppermute | solution.py:568
  53.5 14.6 %all-to-all-start.1 = ((f32[32,5,4,128]{3,2,1,0:T(4,128)}), f32[32,5,4,128]{3,2,1,0:T(4,128)S(1)}, u32[]{:S(2)}, u32[]{:S(2)}) async-start(f32[32,5,4,128]{3,2,1,0:T(4,128)} %bitcast.10), calls=%async_computation.1 | async-start | bytes 655360 | tf_op jit(solution)/shard_map/all_to_all | solution.py:522
  56.1 0.9 %copy-start.6 = (f32[4,48,48]{2,1,0:T(8,128)S(1)}, f32[4,48,48]{2,1,0:T(8,128)}, u32[]{:S(2)}) copy-start(f32[4,48,48]{2,1,0:T(8,128)} %param.18) | copy-start | bytes 110596
  57.0 11.1 %copy-start.15 = (s32[1024]{0:T(1024)S(1)}, s32[1024]{0:T(1024)}, u32[]{:S(2)}) copy-start(s32[1024]{0:T(1024)} %param.19) | copy-start | bytes 12292
  57.0 11.1 %copy-start.17 = (f32[1024]{0:T(1024)S(1)}, f32[1024]{0:T(1024)}, u32[]{:S(2)}) copy-start(f32[1024]{0:T(1024)} %param.20) | copy-start | bytes 12292
